TPU v7x, 32 devices: a whole 2x2x4 slice. The times are simulated.
32 devices in a mesh: frame: 8 (over z, y), row: 4 (over x, core).
Axes of the slice: x: 2, y: 2, z: 4, core: 2. Of those that a mesh axis runs over, the one named last changes fastest.
Arguments:
- features: bfloat16 [16, 64, 64, 640], P('frame', 'row'), may hold values from -6 to 6
- time_weight: bfloat16 [3, 640, 640], replicated, may hold values from -0.125 to 0.125
- time_bias: float32 [640], replicated, may hold values from -3 to 3
- down_weight: bfloat16 [3, 3, 640, 1280], P(None, None, None, 'frame'), may hold values from -0.078125 to 0.078125
- down_bias: float32 [1280], replicated, may hold values from -3 to 3
- norm_gain: float32 [1280], replicated, may hold values from 0.1 to 1.9
- w_query: bfloat16 [1280, 1280], replicated, may hold values from -4 to 4
- w_key: bfloat16 [1280, 1280], replicated, may hold values from -4 to 4
- w_value: bfloat16 [1280, 1280], replicated, may hold values from -0.15625 to 0.15625
- w_out: bfloat16 [1280, 1280], replicated, may hold values from -0.15625 to 0.15625
- out_bias: float32 [1280], replicated, may hold values from -3 to 3
Outputs:
- result: bfloat16 [16, 32, 32, 1280], P('frame', 'row')
All inputs are finite; a program needn't handle non-finite values.
Results may differ from a plain program's by a relative error of at most 0.0085.
Values may be sent and summed in bfloat16 or wider, within the bound.
No kernel may reach another device: no remote copies, remote signals or barrier semaphores. Data moves between devices by JAX's collectives and lax.ppermute only.
A program may use at most 192 MiB of HBM per device.

v0:
```python
import functools

import jax
import jax.numpy as jnp
from jax import lax
from jax.experimental import pallas as pl
from jax.experimental.pallas import tpu as pltpu
from jax.sharding import PartitionSpec as P


HEADS = 16
LANES = 128
MASKED = -3.0e38


def passed_along(value, axis, steps):
    count = lax.axis_size(axis)
    leading, last = (max(0, -steps), min(count, count - steps))
    return lax.ppermute(value, axis, [(source, source + steps) for source in range(leading, last)])


def temporal_kernel(*refs):
    *frame_refs, weight_ref, bias_ref, out_ref, held = refs
    rows, columns, channels = frame_refs[0].shape[1:]
    frames = len(frame_refs) - 2
    count = rows * columns
    values = [ref[...].reshape(count, channels) for ref in frame_refs]
    stacked = [jnp.concatenate(values[tap : tap + frames], axis=0) for tap in range(3)]
    total = jnp.dot(jnp.concatenate(stacked, axis=1), weight_ref[...], preferred_element_type=jnp.float32)
    total = total + (stacked[1].astype(jnp.float32) + bias_ref[...])
    total = total.astype(jnp.bfloat16).astype(jnp.float32)
    lanes = channels // LANES
    for block in range(lanes):
        held[block, 8:, :] = total[:, block * LANES : (block + 1) * LANES]
    half = columns // 2
    first = lax.broadcasted_iota(jnp.int32, (rows * half, LANES), 0) % half == 0
    for place in range(frames):
        for block in range(lanes):
            begin = place * count
            moved = held[block, pl.ds(begin + 7, rows * half, stride=2), :]
            even = held[block, pl.ds(begin + 8, rows * half, stride=2), :]
            odd = held[block, pl.ds(begin + 9, rows * half, stride=2), :]
            moved = jnp.where(first, 0.0, moved)
            for tap, plane in enumerate((moved, even, odd)):
                start = tap * channels + block * LANES
                out_ref[:, place, :, start : start + LANES] = plane.astype(jnp.bfloat16).reshape(
                    rows, half, LANES
                )


def temporal(sequence, time_weight, time_bias, start, rows, step):
    _, _, columns, channels = sequence[0].shape
    frames = len(sequence) - 2
    half = columns // 2
    return pl.pallas_call(
        temporal_kernel,
        out_shape=jax.ShapeDtypeStruct((rows, frames, half, 3 * channels), jnp.bfloat16),
        grid=(rows // step,),
        in_specs=[pl.BlockSpec((1, step, columns, channels), lambda r: (0, r + start // step, 0, 0))]
        * len(sequence)
        + [
            pl.BlockSpec((3 * channels, channels), lambda r: (0, 0)),
            pl.BlockSpec((1, channels), lambda r: (0, 0)),
        ],
        out_specs=pl.BlockSpec((step, frames, half, 3 * channels), lambda r: (r, 0, 0, 0)),
        scratch_shapes=[pltpu.VMEM((channels // LANES, 8 + frames * step * columns, LANES), jnp.float32)],
        cost_estimate=pl.CostEstimate(
            flops=6 * frames * rows * columns * channels * channels,
            bytes_accessed=2 * (5 * frames + 2) * rows * columns * channels,
            transcendentals=0,
        ),
    )(*sequence, time_weight.reshape(3 * channels, channels), time_bias.reshape(1, channels))


def strided_kernel(spans, where_ref, planes_ref, upper_ref, bias_ref, *refs):
    pieces, (*out_refs, weight, total, sems) = refs[: len(spans)], refs[len(spans) :]
    step = pl.program_id(0)
    half_rows, _, frames, half_cols, width = planes_ref.shape
    count = half_rows * frames * half_cols
    channels = width // 3
    _, units, unit, _ = weight.shape

    def copies():
        for place, (piece, (taps, run)) in enumerate(zip(pieces, spans)):
            target = weight.at[pl.ds(where_ref[place, 0], taps), pl.ds(where_ref[place, 1], run)]
            yield pltpu.make_async_copy(piece, target, sems.at[place])

    def product(values, tap):
        result = None
        for part in range(3):
            term = lax.dot_general(
                values[..., part * channels : (part + 1) * channels].reshape(count, channels),
                weight[3 * tap + part].reshape(units * unit, channels),
                (((1,), (1,)), ((), ())),
                preferred_element_type=jnp.float32,
            )
            result = term if result is None else result + term
        return result

    @pl.when(step == 0)
    def _():
        for copy in copies():
            copy.start()
        for copy in copies():
            copy.wait()
        values = jnp.concatenate([upper_ref[...], planes_ref[: half_rows - 1, 1]], axis=0)
        total[...] = product(values, 0) + bias_ref[...]

    @pl.when(step == 1)
    def _():
        total[...] += product(planes_ref[:, 0], 1)

    @pl.when(step == 2)
    def _():
        done = total[...] + product(planes_ref[:, 1], 2)
        done = done.reshape(half_rows, frames, half_cols, done.shape[1])
        part = half_cols // len(out_refs)
        for chunk, out_ref in enumerate(out_refs):
            out_ref[...] = done[:, :, chunk * part : (chunk + 1) * part].astype(jnp.bfloat16)


def strided(planes, upper, pieces, where, bias, chunks):
    rows, frames, half_cols, width = planes.shape
    outputs = bias.shape[0]
    half_rows = rows // 2
    count = half_rows * frames * half_cols
    unit = pieces[0].shape[2]
    channels = width // 3
    block = (half_rows, frames, half_cols // chunks, outputs)
    anywhere = pl.BlockSpec(memory_space=pl.ANY)
    return pl.pallas_call(
        functools.partial(strided_kernel, tuple(piece.shape[:2] for piece in pieces)),
        out_shape=[jax.ShapeDtypeStruct(block, jnp.bfloat16)] * chunks,
        grid=(3,),
        in_specs=[
            pl.BlockSpec(memory_space=pltpu.SMEM),
            pl.BlockSpec((half_rows, 2, frames, half_cols, width), lambda a: (0, 0, 0, 0, 0)),
            pl.BlockSpec((1, frames, half_cols, width), lambda a: (0, 0, 0, 0)),
            pl.BlockSpec((1, outputs), lambda a: (0, 0)),
        ]
        + [anywhere] * len(pieces),
        out_specs=[pl.BlockSpec(block, lambda a: (0, 0, 0, 0))] * chunks,
        scratch_shapes=[
            pltpu.VMEM((9, outputs // unit, unit, channels), jnp.bfloat16),
            pltpu.VMEM((count, outputs), jnp.float32),
            pltpu.SemaphoreType.DMA((len(pieces),)),
        ],
        cost_estimate=pl.CostEstimate(
            flops=6 * count * width * outputs,
            bytes_accessed=2 * (planes.size + 3 * width * outputs + count * outputs),
            transcendentals=0,
        ),
    )(
        where,
        planes.reshape(half_rows, 2, frames, half_cols, width),
        upper,
        bias.reshape(1, outputs),
        *pieces,
    )


def attention_kernel(
    tokens_ref, gain_ref, bias_ref, wq_hbm, wk_hbm, wv_hbm, wo_hbm, out_ref,
    wq, wk, wv, wo, held, normed, query, key, value, sems,
):
    copies = []
    for place, (source, target) in enumerate(((wq_hbm, wq), (wk_hbm, wk), (wv_hbm, wv), (wo_hbm, wo))):
        copies.append(pltpu.make_async_copy(source, target, sems.at[place]))
        copies[-1].start()
    frames, pixels, width = out_ref.shape
    groups = pixels // 8
    rows = frames * 8
    sources, span, _, half_width = tokens_ref.shape
    share = half_width // (sources // 2)
    head_width = width // HEADS
    scale = head_width ** (-0.5)
    for group in range(groups):
        here = slice(group * 8, group * 8 + 8)
        low = [tokens_ref[2 * line, :, here, :] for line in range(sources // 2)]
        high = [tokens_ref[2 * line + 1, span - 1 - at, here, :] for line in range(sources // 2) for at in range(span)]
        low = jnp.concatenate([value.astype(jnp.float32).reshape(span * 8, half_width) for value in low], axis=0)
        high = jnp.concatenate([value.astype(jnp.float32) for value in high], axis=0)
        parts = []
        for line in range(sources // 2):
            parts += [low[:, line * share : (line + 1) * share], high[:, line * share : (line + 1) * share]]
        tokens = jnp.concatenate(parts, axis=1)
        held[group * rows : (group + 1) * rows, :] = tokens.astype(jnp.bfloat16)
        centred = tokens - jnp.mean(tokens, axis=-1, keepdims=True)
        spread = jnp.mean(centred * centred, axis=-1, keepdims=True)
        result = centred * lax.rsqrt(spread + 1e-05) * gain_ref[...]
        normed[group * rows : (group + 1) * rows, :] = result.astype(jnp.bfloat16)
    step = 256
    for place, (weight, target) in enumerate(((wq, query), (wk, key), (wv, value))):
        copies[place].wait()

        @pl.loop(0, width // step)
        def _(n):
            part = pl.ds(pl.multiple_of(n * step, step), step)
            target[:, part] = jnp.dot(
                normed[...], weight[:, part], preferred_element_type=jnp.float32
            ).astype(jnp.bfloat16)

    same = (
        lax.broadcasted_iota(jnp.int32, (rows, rows), 0) % 8
        == lax.broadcasted_iota(jnp.int32, (rows, rows), 1) % 8
    )

    @pl.loop(0, groups)
    def _(group):
        here = pl.ds(pl.multiple_of(group * rows, rows), rows)
        sums = [None] * (width // LANES)
        for head in range(HEADS):
            low = head * head_width // LANES
            high = ((head + 1) * head_width - 1) // LANES + 1
            window = slice(low * LANES, high * LANES)
            lane = lax.broadcasted_iota(jnp.int32, (rows, (high - low) * LANES), 1) + low * LANES
            mine = (lane >= head * head_width) & (lane < (head + 1) * head_width)
            zeros = jnp.zeros((rows, (high - low) * LANES), jnp.bfloat16)
            queries = jnp.where(mine, query[here, window], zeros)
            scores = lax.dot_general(
                queries, key[here, window], (((1,), (1,)), ((), ())), preferred_element_type=jnp.float32
            )
            scores = jnp.where(same, scores * scale, MASKED)
            powers = jnp.exp(scores - jnp.max(scores, axis=-1, keepdims=True))
            weights = powers * (1.0 / jnp.sum(powers, axis=-1, keepdims=True))
            values = jnp.where(mine, value[here, window], zeros)
            part = jnp.dot(weights.astype(jnp.bfloat16), values, preferred_element_type=jnp.float32)
            for block in range(low, high):
                piece = part[:, (block - low) * LANES : (block - low + 1) * LANES]
                sums[block] = piece if sums[block] is None else sums[block] + piece
        for block, total in enumerate(sums):
            normed[here, block * LANES : (block + 1) * LANES] = total.astype(jnp.bfloat16)

    copies[3].wait()

    @pl.loop(0, width // step)
    def _(n):
        part = pl.ds(pl.multiple_of(n * step, step), step)
        output = jnp.dot(normed[...], wo[:, part], preferred_element_type=jnp.float32)
        output = output + bias_ref[:, part]
        for group in range(groups):
            here = slice(group * rows, (group + 1) * rows)
            piece = (output[here] + held[here, part].astype(jnp.float32)).reshape(frames, 8, step)
            out_ref[:, group * 8 : group * 8 + 8, part] = piece.astype(jnp.bfloat16)


def attention(tokens, norm_gain, out_bias, w_query, w_key, w_value, w_out):
    sources, span, pixels, half_width = tokens.shape
    frames, width = sources * span // 2, 2 * half_width
    count = frames * pixels
    weight = pltpu.VMEM((width, width), jnp.bfloat16)
    rows = pltpu.VMEM((count, width), jnp.bfloat16)
    anywhere = pl.BlockSpec(memory_space=pl.ANY)
    inside = pl.BlockSpec(memory_space=pltpu.VMEM)
    return pl.pallas_call(
        attention_kernel,
        out_shape=jax.ShapeDtypeStruct((frames, pixels, width), jnp.bfloat16),
        in_specs=[inside, inside, inside, anywhere, anywhere, anywhere, anywhere],
        out_specs=inside,
        scratch_shapes=[weight] * 4 + [rows] * 5 + [pltpu.SemaphoreType.DMA((4,))],
        cost_estimate=pl.CostEstimate(
            flops=8 * count * width * width,
            bytes_accessed=8 * width * width + 4 * count * width,
            transcendentals=count * HEADS * frames * 8,
        ),
    )(
        tokens, norm_gain.reshape(1, width), out_bias.reshape(1, width), w_query, w_key, w_value, w_out
    )


def on_device(
    features,
    time_weight,
    time_bias,
    down_weight,
    down_bias,
    norm_gain,
    w_query,
    w_key,
    w_value,
    w_out,
    out_bias,
):
    frames_here, rows_here, columns, channels = features.shape
    groups = lax.axis_size("frame")
    lines = groups // 2
    frame, row = lax.axis_index("frame"), lax.axis_index("row")
    side = frame % 2

    everyone = range(groups)
    swapped = [(at, at ^ 1) for at in everyone]
    own = [
        lax.dynamic_slice_in_dim(features, jnp.where(side == 0, at, frames_here - 1 - at), 1, axis=0)
        for at in range(frames_here)
    ]
    other = [lax.ppermute(own[0], "frame", swapped)]
    later = list(own[1:])
    other[0], *later = lax.optimization_barrier([other[0]] + later)
    other += [lax.ppermute(value, "frame", swapped) for value in later]
    outward = [(at, at + (2 if at % 2 else -2)) for at in everyone]
    inward = [(at, at + (-2 if at % 2 else 2)) for at in everyone]
    inside = lambda pairs: [(source, target) for source, target in pairs if 0 <= target < groups]
    last = lax.ppermute(own[0], "frame", inside(outward))
    first = lax.ppermute(other[0], "frame", inside(inward))
    sequence = [first] + own + other[::-1] + [last]

    pieces, where, distant = strided_weights(down_weight, frame, row, channels)

    taps = jnp.where(side == 0, time_weight, time_weight[::-1])
    final = temporal(sequence, taps, time_bias, rows_here - 1, 1, 1)
    upper = passed_along(final, "row", 1)
    planes = temporal(sequence, taps, time_bias, 0, rows_here, 2)
    shares = down_bias.reshape(lines, 2, down_bias.shape[0] // groups)
    bias = lax.dynamic_index_in_dim(shares, side, axis=1, keepdims=False).reshape(-1)
    planes, *distant = lax.optimization_barrier([planes] + distant)
    pieces += [lax.ppermute(value, "row", [(at, at ^ 1) for at in range(lax.axis_size("row"))]) for value in distant]

    half_rows, half_cols = rows_here // 2, columns // 2
    pixels_here = half_rows * half_cols // groups
    chunks = 2 if groups == half_rows and pixels_here % 16 == 0 else 1
    results = []
    for coarse in strided(planes, upper, pieces, where, bias, chunks):
        half_width = coarse.shape[-1]
        part = pixels_here // chunks
        tokens = coarse
        if groups != half_rows:
            tokens = tokens.transpose(1, 0, 2, 3).reshape(2 * frames_here, groups, part, half_width)
            tokens = tokens.transpose(1, 0, 2, 3)
        moved = lax.all_to_all(tokens, "frame", split_axis=0, concat_axis=0, tiled=True)
        result = attention(moved, norm_gain, out_bias, w_query, w_key, w_value, w_out)
        result = result.reshape(groups, frames_here, part, 2 * half_width)
        results.append(lax.all_to_all(result, "frame", split_axis=0, concat_axis=0, tiled=True))
    returned = jnp.concatenate(results, axis=2).transpose(1, 0, 2, 3)
    return returned.reshape(frames_here, half_rows, half_cols, 2 * half_width)


def strided_weights(down_weight, frame, row, channels):
    groups, row_devices = lax.axis_size("frame"), lax.axis_size("row")
    lines = groups // 2
    share = down_weight.shape[3]
    line = frame // 2
    shard = down_weight.transpose(0, 1, 3, 2).reshape(9, share, channels)
    unit = share // 2
    if unit % 16 or lines & (lines - 1) or row_devices % 4:
        members = [[2 * at + side for at in range(lines)] for side in range(2)]
        gathered = lax.all_gather(shard, "frame", axis=1, tiled=True, axis_index_groups=members)
        return [gathered[:, None]], jnp.zeros((1, 2), jnp.int32), []
    core, plane = row % 2, row // 2 % 2
    shard = shard.reshape(9, 2, unit, channels)
    pieces, where, distant, beyond = [shard], [(0, 2 * line)], [], []
    mine = lax.dynamic_slice(shard, (4 * plane, core, 0, 0), (5, 1, unit, channels))
    rows = range(row_devices)
    for distance in range(1, lines):
        place = 2 * (line ^ distance)
        steps = [(at, (at // 2 ^ distance) * 2 + at % 2) for at in range(groups)]
        near = lax.ppermute(mine, "frame", steps)
        sent = lax.dynamic_slice_in_dim(near, plane, 4, axis=0)
        far = lax.ppermute(sent, "row", [(at, at ^ 2) for at in rows])
        pieces += [near, far, lax.ppermute(near, "row", [(at, at ^ 1) for at in rows])]
        where += [(4 * plane, place + core), (5 - 5 * plane, place + core), (4 * plane, place + 1 - core)]
        distant.append(far)
        beyond.append((5 - 5 * plane, place + 1 - core))
    where = jnp.stack([jnp.stack([jnp.int32(tap), jnp.int32(at)]) for tap, at in where + beyond])
    return pieces, where, distant


def solution(mesh):
    return jax.shard_map(
        on_device,
        mesh=mesh,
        in_specs=(
            P("frame", "row", None, None),
            P(),
            P(),
            P(None, None, None, "frame"),
            P(),
            P(),
            P(),
            P(),
            P(),
            P(),
            P(),
        ),
        out_specs=P("frame", "row", None, None),
        check_vma=False,
    )
```

profile of v0, /device:TPU:0, one launch (start us, length us, event | category | flops | bytes accessed | tf_op | source)
XLA Modules:
  0.0 258.8 jit_solution(4912672859089641594)
XLA Ops:
  0.0 1.9 constant_dynamic-slice_fusion.4
  2.0 3.1 %collective-permute-start = (bf16[1,16,64,640]{3,2,1,0:T(8,128)(2,1)S(1)}, bf16[1,16,64,640]{3,2,1,0:T(8,128)(2,1)}, u32[]{:S(2)}, u32[]{:S(2)}) collective-permute-start(bf16[1,16,64,640]{3,2,1,0:T(8,128)(2,1)S(1)} %get-tuple-element.22.refs_1_), channel_id=1, source_target_pairs={{0,4},{4,0},{8,12},{12,8},{16,20},{20,16},{24,28},{28,24},{1,5},{5... | collective-permute-start | bytes 3932168 | tf_op jit(solution)/shard_map/ppermute | solution.py:296
  5.0 1.1 constant_dynamic-slice_fusion.3
  6.1 1.6 collective-permute-start.4
  7.8 1.3 collective-permute-start.3
  9.0 24.9 %collective-permute-done.refs_4_ = bf16[1,16,64,640]{3,2,1,0:T(8,128)(2,1)} collective-permute-done((bf16[1,16,64,640]{3,2,1,0:T(8,128)(2,1)S(1)}, bf16[1,16,64,640]{3,2,1,0:T(8,128)(2,1)}, u32[]{:S(2)}, u32[]{:S(2)}) %collective-permute-start) | collective-permute-done | bytes 1310752 | tf_op jit(solution)/shard_map/ppermute | solution.py:296
  33.9 4.8 %collective-permute-start.1 = (bf16[1,16,64,640]{3,2,1,0:T(8,128)(2,1)}, bf16[1,16,64,640]{3,2,1,0:T(8,128)(2,1)}, u32[]{:S(2)}, u32[]{:S(2)}) collective-permute-start(bf16[1,16,64,640]{3,2,1,0:T(8,128)(2,1)} %collective-permute-done.refs_4_), channel_id=1, source_target_pairs={{0,8},{8,16},{12,4},{16,24},{20,12},{28,20},{1,9},{9,17},{13,5},{1... | collective-permute-start | bytes 3932168 | tf_op jit(solution)/shard_map/ppermute | solution.py:304
  38.7 2.0 collective-permute-start.6
  40.7 2.1 collective-permute-start.8
  42.7 4.5 %reverse_select_fusion = bf16[3,640,640]{2,1,0:T(8,128)(2,1)} fusion(bf16[3,640,640]{2,1,0:T(8,128)(2,1)} %param.12, pred[]{:T(512)S(6)} %eq.9), kind=kLoop, calls=%fused_computation | loop fusion | flops 1228800 | bytes 4915201 | tf_op jit(solution)/shard_map/jit(_where)/select_n | solution.py:309
  47.3 1.0 constant_dynamic-slice_fusion.2
  48.3 29.7 %collective-permute-done.6.refs_4_ = bf16[5,1,80,640]{3,2,1,0:T(8,128)(2,1)} collective-permute-done((bf16[5,1,80,640]{3,2,1,0:T(8,128)(2,1)S(1)}, bf16[5,1,80,640]{3,2,1,0:T(8,128)(2,1)}, u32[]{:S(2)}, u32[]{:S(2)}) %collective-permute-start.6) | collective-permute-done | bytes 512032 | tf_op jit(solution)/shard_map/ppermute | solution.py:356
  78.0 1.5 collective-permute-start.5
  79.5 1.8 constant_dynamic-slice_fusion.1
  81.3 5.7 %collective-permute-done.8.refs_7_ = bf16[5,1,80,640]{3,2,1,0:T(8,128)(2,1)S(1)} collective-permute-done((bf16[5,1,80,640]{3,2,1,0:T(8,128)(2,1)S(1)}, bf16[5,1,80,640]{3,2,1,0:T(8,128)(2,1)S(1)}, u32[]{:S(2)}, u32[]{:S(2)}) %collective-permute-start.8) | collective-permute-done | bytes 512032 | tf_op jit(solution)/shard_map/ppermute | solution.py:356
  87.0 0.8 copy-done.3
  87.8 1.5 collective-permute-start.7
  90.8 1.0 constant_dynamic-slice_fusion
  93.0 3.9 %shard_map.110 = bf16[1,4,32,1920]{3,2,1,0:T(8,128)(2,1)} custom-call(bf16[1,16,64,640]{3,2,1,0:T(8,128)(2,1)} %collective-permute-done.1.refs_0_, bf16[1,16,64,640]{3,2,1,0:T(8,128)(2,1)} %copy-done.1, bf16[1,16,64,640]{3,2,1,0:T(8,128)(2,1)} %copy-done, bf16[1,16,64,640]{3,2,1,0:T(8,128)(2,1)} %collective-permute-done.2.refs_3_, ...), custom_call_target="tpu_custom_call" | custom-call | flops 629145600 | bytes 1802240 | tf_op jit(solution)/shard_map/pallas_call | solution.py:55
  97.0 3.4 %collective-permute-done.7.refs_5_ = bf16[4,1,80,640]{3,2,1,0:T(8,128)(2,1)} collective-permute-done((bf16[4,1,80,640]{3,2,1,0:T(8,128)(2,1)}, bf16[4,1,80,640]{3,2,1,0:T(8,128)(2,1)}, u32[]{:S(2)}, u32[]{:S(2)}) %collective-permute-start.7) | collective-permute-done | bytes 409632 | tf_op jit(solution)/shard_map/ppermute | solution.py:358
  100.4 1.5 collective-permute-start.10
  101.9 18.7 %shard_map.109 = bf16[16,4,32,1920]{3,2,1,0:T(8,128)(2,1)} custom-call(bf16[1,16,64,640]{3,2,1,0:T(8,128)(2,1)} %collective-permute-done.1.refs_0_, bf16[1,16,64,640]{3,2,1,0:T(8,128)(2,1)} %copy-done.1, bf16[1,16,64,640]{3,2,1,0:T(8,128)(2,1)} %copy-done, bf16[1,16,64,640]{3,2,1,0:T(8,128)(2,1)} %collective-permute-done.2.refs_3_, ...), custom_call_target="tpu_custom_call" | custom-call | flops 10066329600 | bytes 28835840 | tf_op jit(solution)/shard_map/pallas_call | solution.py:55
  120.7 2.3 collective-permute-start.14
  123.8 1.2 stack.159.where_ref
  126.6 18.8 %shard_map.111 = (bf16[8,4,16,640]{3,2,1,0:T(8,128)(2,1)}, bf16[8,4,16,640]{3,2,1,0:T(8,128)(2,1)}) custom-call(s32[13,2]{1,0:T(8,128)} %stack.159.where_ref, bf16[8,2,4,32,1920]{4,3,2,1,0:T(8,128)(2,1)} %bitcast.50, bf16[1,4,32,1920]{3,2,1,0:T(8,128)(2,1)} %copy-done.12, f32[1,640]{1,0:T(1,128)} %reshape_reshape.7.bias_ref, ...), custom_call_target="tpu_custom_call" | custom-call | flops 7549747200 | bytes 16547840 | tf_op jit(solution)/shard_map/pallas_call | solution.py:131
  145.4 45.1 %all_to_all.20.tokens_ref = bf16[8,4,16,640]{3,2,1,0:T(8,128)(2,1)} all-to-all(bf16[8,4,16,640]{3,2,1,0:T(8,128)(2,1)} %get-tuple-element.19), channel_id=1, replica_groups=mesh['frame'=8,'row'=4] {'frame'}, dimensions={0} | all-to-all | bytes 1310720 | tf_op jit(solution)/shard_map/all_to_all | solution.py:329
  190.5 3.8 %all-to-all-start.2 = ((bf16[8,4,16,640]{3,2,1,0:T(8,128)(2,1)}), bf16[8,4,16,640]{3,2,1,0:T(8,128)(2,1)S(1)}, u32[]{:S(2)}, u32[]{:S(2)}) async-start(bf16[8,4,16,640]{3,2,1,0:T(8,128)(2,1)} %get-tuple-element.20), calls=%async_computation.2 | async-start | bytes 1310720 | tf_op jit(solution)/shard_map/all_to_all | solution.py:329
  195.4 16.8 %shard_map.112 = bf16[16,16,1280]{2,1,0:T(8,128)(2,1)} custom-call(bf16[8,4,16,640]{3,2,1,0:T(8,128)(2,1)} %all_to_all.20.tokens_ref, f32[1,1280]{1,0:T(1,128)} %reshape.33.gain_ref, f32[1,1280]{1,0:T(1,128)} %reshape.34.bias_ref, bf16[1280,1280]{1,0:T(8,128)(2,1)} %wq_hbm.3, bf16[1280,1280]{1,0:T(8,128)(2,1)} %wk_hbm.3, bf16[1280,1280]{1,0:T(8,128)(2,1)} %wv_hbm.3, ...), custom_call_target="tpu_custom_call" | custom-call | flops 3355443200 | bytes 14417920 | tf_op jit(solution)/shard_map/pallas_call | solution.py:255
  212.3 5.7 %all-to-all-start.1 = ((bf16[8,2,16,1280]{3,2,1,0:T(8,128)(2,1)}), bf16[8,2,16,1280]{3,2,1,0:T(8,128)(2,1)S(1)}, u32[]{:S(2)}, u32[]{:S(2)}) async-start(bf16[8,2,16,1280]{3,2,1,0:T(8,128)(2,1)} %bitcast.46), calls=%async_computation.1 | async-start | bytes 1310720 | tf_op jit(solution)/shard_map/all_to_all | solution.py:332
  218.0 16.9 %shard_map.113 = bf16[16,16,1280]{2,1,0:T(8,128)(2,1)} custom-call(bf16[8,4,16,640]{3,2,1,0:T(8,128)(2,1)} %copy-done.2, f32[1,1280]{1,0:T(1,128)} %reshape.33.gain_ref, f32[1,1280]{1,0:T(1,128)} %reshape.34.bias_ref, bf16[1280,1280]{1,0:T(8,128)(2,1)} %wq_hbm.3, bf16[1280,1280]{1,0:T(8,128)(2,1)} %wk_hbm.3, bf16[1280,1280]{1,0:T(8,128)(2,1)} %wv_hbm.3, ...), custom_call_target="tpu_custom_call" | custom-call | flops 3355443200 | bytes 14417920 | tf_op jit(solution)/shard_map/pallas_call | solution.py:255
  234.9 22.7 %all_to_all.21 = bf16[8,2,16,1280]{3,2,1,0:T(8,128)(2,1)S(1)} all-to-all(bf16[8,2,16,1280]{3,2,1,0:T(8,128)(2,1)} %bitcast.47), channel_id=1, replica_groups=mesh['frame'=8,'row'=4] {'frame'}, dimensions={0} | all-to-all | bytes 1310720 | tf_op jit(solution)/shard_map/all_to_all | solution.py:332
  257.7 1.1 copy.31
  (63 shorter events, 6.6 us)
Async XLA Ops:
  1.9 45.3 %copy-start = (bf16[1,16,64,640]{3,2,1,0:T(8,128)(2,1)}, bf16[1,16,64,640]{3,2,1,0:T(8,128)(2,1)S(1)}, u32[]{:S(2)}) copy-start(bf16[1,16,64,640]{3,2,1,0:T(8,128)(2,1)S(1)} %get-tuple-element.14.refs_2_) | copy-start | bytes 3932164
  2.0 45.3 %copy-start.1 = (bf16[1,16,64,640]{3,2,1,0:T(8,128)(2,1)}, bf16[1,16,64,640]{3,2,1,0:T(8,128)(2,1)S(1)}, u32[]{:S(2)}) copy-start(bf16[1,16,64,640]{3,2,1,0:T(8,128)(2,1)S(1)} %get-tuple-element.22.refs_1_) | copy-start | bytes 3932164
  2.0 31.9 %collective-permute-start = (bf16[1,16,64,640]{3,2,1,0:T(8,128)(2,1)S(1)}, bf16[1,16,64,640]{3,2,1,0:T(8,128)(2,1)}, u32[]{:S(2)}, u32[]{:S(2)}) collective-permute-start(bf16[1,16,64,640]{3,2,1,0:T(8,128)(2,1)S(1)} %get-tuple-element.22.refs_1_), channel_id=1, source_target_pairs={{0,4},{4,0},{8,12},{12,8},{16,20},{20,16},{24,28},{28,24},{1,5},{5... | collective-permute-start | bytes 3932168 | tf_op jit(solution)/shard_map/ppermute | solution.py:296
  6.1 34.6 %collective-permute-start.4 = (bf16[5,1,80,640]{3,2,1,0:T(8,128)(2,1)S(1)}, bf16[5,1,80,640]{3,2,1,0:T(8,128)(2,1)}, u32[]{:S(2)}, u32[]{:S(2)}) collective-permute-start(bf16[5,1,80,640]{3,2,1,0:T(8,128)(2,1)S(1)} %constant_dynamic-slice_fusion.3), channel_id=1, source_target_pairs={{0,8},{4,12},{8,0},{12,4},{16,24},{20,28},{24,16},{28,20},{1,9},{5... | collective-permute-start | bytes 1536008 | tf_op jit(solution)/shard_map/ppermute | solution.py:356
  7.8 84.1 %collective-permute-start.3 = (bf16[1,16,64,640]{3,2,1,0:T(8,128)(2,1)S(1)}, bf16[1,16,64,640]{3,2,1,0:T(8,128)(2,1)}, u32[]{:S(2)}, u32[]{:S(2)}) collective-permute-start(bf16[1,16,64,640]{3,2,1,0:T(8,128)(2,1)S(1)} %get-tuple-element.22.refs_1_), channel_id=1, source_target_pairs={{4,12},{8,0},{12,20},{16,8},{20,28},{24,16},{5,13},{9,1},{13,21},{... | collective-permute-start | bytes 3932168 | tf_op jit(solution)/shard_map/ppermute | solution.py:303
  33.9 58.6 %collective-permute-start.1 = (bf16[1,16,64,640]{3,2,1,0:T(8,128)(2,1)}, bf16[1,16,64,640]{3,2,1,0:T(8,128)(2,1)}, u32[]{:S(2)}, u32[]{:S(2)}) collective-permute-start(bf16[1,16,64,640]{3,2,1,0:T(8,128)(2,1)} %collective-permute-done.refs_4_), channel_id=1, source_target_pairs={{0,8},{8,16},{12,4},{16,24},{20,12},{28,20},{1,9},{9,17},{13,5},{1... | collective-permute-start | bytes 3932168 | tf_op jit(solution)/shard_map/ppermute | solution.py:304
  38.7 53.8 %collective-permute-start.2 = (bf16[1,16,64,640]{3,2,1,0:T(8,128)(2,1)S(1)}, bf16[1,16,64,640]{3,2,1,0:T(8,128)(2,1)}, u32[]{:S(2)}, u32[]{:S(2)}) collective-permute-start(bf16[1,16,64,640]{3,2,1,0:T(8,128)(2,1)S(1)} %get-tuple-element.14.refs_2_), channel_id=1, source_target_pairs={{0,4},{4,0},{8,12},{12,8},{16,20},{20,16},{24,28},{28,24},{1,5},{5... | collective-permute-start | bytes 3932168 | tf_op jit(solution)/shard_map/ppermute | solution.py:299
  38.7 39.3 %collective-permute-start.6 = (bf16[5,1,80,640]{3,2,1,0:T(8,128)(2,1)S(1)}, bf16[5,1,80,640]{3,2,1,0:T(8,128)(2,1)}, u32[]{:S(2)}, u32[]{:S(2)}) collective-permute-start(bf16[5,1,80,640]{3,2,1,0:T(8,128)(2,1)S(1)} %constant_dynamic-slice_fusion.3), channel_id=1, source_target_pairs={{0,16},{4,20},{8,24},{12,28},{16,0},{20,4},{24,8},{28,12},{1,17},{... | collective-permute-start | bytes 1536008 | tf_op jit(solution)/shard_map/ppermute | solution.py:356
  40.7 48.7 %copy-start.8 = (f32[640]{0:T(1024)S(1)}, f32[640]{0:T(1024)}, u32[]{:S(2)}) copy-start(f32[640]{0:T(1024)} %param.13) | copy-start | bytes 7684
  40.7 49.3 %copy-start.5 = (f32[1280]{0:T(1024)S(1)}, f32[1280]{0:T(1024)}, u32[]{:S(2)}) copy-start(f32[1280]{0:T(1024)} %param.15) | copy-start | bytes 15364
  40.7 46.3 %collective-permute-start.8 = (bf16[5,1,80,640]{3,2,1,0:T(8,128)(2,1)S(1)}, bf16[5,1,80,640]{3,2,1,0:T(8,128)(2,1)S(1)}, u32[]{:S(2)}, u32[]{:S(2)}) collective-permute-start(bf16[5,1,80,640]{3,2,1,0:T(8,128)(2,1)S(1)} %constant_dynamic-slice_fusion.3), channel_id=1, source_target_pairs={{0,24},{4,28},{8,16},{12,20},{16,8},{20,12},{24,0},{28,4},{1,25},{... | collective-permute-start | bytes 1536008 | tf_op jit(solution)/shard_map/ppermute | solution.py:356
  78.0 18.9 %collective-permute-start.5 = (bf16[4,1,80,640]{3,2,1,0:T(8,128)(2,1)S(1)}, bf16[4,1,80,640]{3,2,1,0:T(8,128)(2,1)}, u32[]{:S(2)}, u32[]{:S(2)}) collective-permute-start(bf16[4,1,80,640]{3,2,1,0:T(8,128)(2,1)S(1)} %constant_dynamic-slice_fusion.2), channel_id=1, source_target_pairs={{0,2},{1,3},{2,0},{3,1},{4,6},{5,7},{6,4},{7,5},{8,10},{9,11},{10,... | collective-permute-start | bytes 1228808 | tf_op jit(solution)/shard_map/ppermute | solution.py:358
  87.8 12.7 %collective-permute-start.7 = (bf16[4,1,80,640]{3,2,1,0:T(8,128)(2,1)}, bf16[4,1,80,640]{3,2,1,0:T(8,128)(2,1)}, u32[]{:S(2)}, u32[]{:S(2)}) collective-permute-start(bf16[4,1,80,640]{3,2,1,0:T(8,128)(2,1)} %constant_dynamic-slice_fusion.1), channel_id=1, source_target_pairs={{0,2},{1,3},{2,0},{3,1},{4,6},{5,7},{6,4},{7,5},{8,10},{9,11},{10,... | collective-permute-start | bytes 1228808 | tf_op jit(solution)/shard_map/ppermute | solution.py:358
  91.9 28.8 %collective-permute-start.9 = (bf16[4,1,80,640]{3,2,1,0:T(8,128)(2,1)S(1)}, bf16[4,1,80,640]{3,2,1,0:T(8,128)(2,1)}, u32[]{:S(2)}, u32[]{:S(2)}) collective-permute-start(bf16[4,1,80,640]{3,2,1,0:T(8,128)(2,1)S(1)} %constant_dynamic-slice_fusion), channel_id=1, source_target_pairs={{0,2},{1,3},{2,0},{3,1},{4,6},{5,7},{6,4},{7,5},{8,10},{9,11},{10,... | collective-permute-start | bytes 1228808 | tf_op jit(solution)/shard_map/ppermute | solution.py:358
  92.5 30.4 %collective-permute-start.11 = (bf16[5,1,80,640]{3,2,1,0:T(8,128)(2,1)}, bf16[5,1,80,640]{3,2,1,0:T(8,128)(2,1)S(1)}, u32[]{:S(2)}, u32[]{:S(2)}) collective-permute-start(bf16[5,1,80,640]{3,2,1,0:T(8,128)(2,1)} %collective-permute-done.4.refs_1_), channel_id=1, source_target_pairs={{0,1},{1,0},{2,3},{3,2},{4,5},{5,4},{6,7},{7,6},{8,9},{9,8},{10,11... | collective-permute-start | bytes 1536008 | tf_op jit(solution)/shard_map/ppermute | solution.py:359
  92.5 30.5 %collective-permute-start.12 = (bf16[5,1,80,640]{3,2,1,0:T(8,128)(2,1)}, bf16[5,1,80,640]{3,2,1,0:T(8,128)(2,1)S(1)}, u32[]{:S(2)}, u32[]{:S(2)}) collective-permute-start(bf16[5,1,80,640]{3,2,1,0:T(8,128)(2,1)} %collective-permute-done.6.refs_4_), channel_id=1, source_target_pairs={{0,1},{1,0},{2,3},{3,2},{4,5},{5,4},{6,7},{7,6},{8,9},{9,8},{10,11... | collective-permute-start | bytes 1536008 | tf_op jit(solution)/shard_map/ppermute | solution.py:359
  93.0 3.9 %copy-start.4 = (bf16[5,1,80,640]{3,2,1,0:T(8,128)(2,1)S(1)}, bf16[5,1,80,640]{3,2,1,0:T(8,128)(2,1)}, u32[]{:S(2)}) copy-start(bf16[5,1,80,640]{3,2,1,0:T(8,128)(2,1)} %copy-done.3) | copy-start | bytes 1536004
  96.9 28.1 %collective-permute-start.13 = (bf16[5,1,80,640]{3,2,1,0:T(8,128)(2,1)S(1)}, bf16[5,1,80,640]{3,2,1,0:T(8,128)(2,1)S(1)}, u32[]{:S(2)}, u32[]{:S(2)}) collective-permute-start(bf16[5,1,80,640]{3,2,1,0:T(8,128)(2,1)S(1)} %copy-done.4), channel_id=1, source_target_pairs={{0,1},{1,0},{2,3},{3,2},{4,5},{5,4},{6,7},{7,6},{8,9},{9,8},{10,11... | collective-permute-start | bytes 1536008 | tf_op jit(solution)/shard_map/ppermute | solution.py:359
  100.4 25.4 %collective-permute-start.10 = (bf16[1,4,32,1920]{3,2,1,0:T(8,128)(2,1)}, bf16[1,4,32,1920]{3,2,1,0:T(8,128)(2,1)S(1)}, u32[]{:S(2)}, u32[]{:S(2)}) collective-permute-start(bf16[1,4,32,1920]{3,2,1,0:T(8,128)(2,1)} %shard_map.110), channel_id=1, source_target_pairs={{0,1},{1,2},{2,3},{4,5},{5,6},{6,7},{8,9},{9,10},{10,11},{12,13},{... | collective-permute-start | bytes 1474568 | tf_op jit(solution)/shard_map/ppermute | solution.py:19
  120.7 4.3 %collective-permute-start.14 = (bf16[4,1,80,640]{3,2,1,0:T(8,128)(2,1)}, bf16[4,1,80,640]{3,2,1,0:T(8,128)(2,1)S(1)}, u32[]{:S(2)}, u32[]{:S(2)}) collective-permute-start(bf16[4,1,80,640]{3,2,1,0:T(8,128)(2,1)} %collective-permute-done.5.refs_2_), channel_id=1, source_target_pairs={{0,1},{1,0},{2,3},{3,2},{4,5},{5,4},{6,7},{7,6},{8,9},{9,8},{10,11... | collective-permute-start | bytes 1228808 | tf_op jit(solution)/shard_map/ppermute | solution.py:316
  122.9 2.9 %copy-start.9 = (bf16[5,1,80,640]{3,2,1,0:T(8,128)(2,1)}, bf16[5,1,80,640]{3,2,1,0:T(8,128)(2,1)S(1)}, u32[]{:S(2)}) copy-start(bf16[5,1,80,640]{3,2,1,0:T(8,128)(2,1)S(1)} %collective-permute-done.11.refs_3_) | copy-start | bytes 1536004
  122.9 2.3 collective-permute-start.15
  123.0 2.8 %copy-start.10 = (bf16[5,1,80,640]{3,2,1,0:T(8,128)(2,1)}, bf16[5,1,80,640]{3,2,1,0:T(8,128)(2,1)S(1)}, u32[]{:S(2)}) copy-start(bf16[5,1,80,640]{3,2,1,0:T(8,128)(2,1)S(1)} %collective-permute-done.12.refs_6_) | copy-start | bytes 1536004
  123.0 2.8 %collective-permute-start.16 = (bf16[4,1,80,640]{3,2,1,0:T(8,128)(2,1)}, bf16[4,1,80,640]{3,2,1,0:T(8,128)(2,1)}, u32[]{:S(2)}, u32[]{:S(2)}) collective-permute-start(bf16[4,1,80,640]{3,2,1,0:T(8,128)(2,1)} %collective-permute-done.9.refs_8_), channel_id=1, source_target_pairs={{0,1},{1,0},{2,3},{3,2},{4,5},{5,4},{6,7},{7,6},{8,9},{9,8},{10,11... | collective-permute-start | bytes 1228808 | tf_op jit(solution)/shard_map/ppermute | solution.py:316
  125.0 0.9 copy-start.11
  125.0 0.9 copy-start.13
  125.8 0.8 copy-start.12
  145.4 48.9 %copy-start.6 = (f32[1280]{0:T(1024)S(1)}, f32[1280]{0:T(1024)}, u32[]{:S(2)}) copy-start(f32[1280]{0:T(1024)} %param.16) | copy-start | bytes 15364
  145.4 49.4 %copy-start.7 = (f32[1280]{0:T(1024)S(1)}, f32[1280]{0:T(1024)}, u32[]{:S(2)}) copy-start(f32[1280]{0:T(1024)} %param.21) | copy-start | bytes 15364
  190.5 21.8 %all-to-all-start.2 = ((bf16[8,4,16,640]{3,2,1,0:T(8,128)(2,1)}), bf16[8,4,16,640]{3,2,1,0:T(8,128)(2,1)S(1)}, u32[]{:S(2)}, u32[]{:S(2)}) async-start(bf16[8,4,16,640]{3,2,1,0:T(8,128)(2,1)} %get-tuple-element.20), calls=%async_computation.2 | async-start | bytes 1310720 | tf_op jit(solution)/shard_map/all_to_all | solution.py:329
  212.3 5.7 %copy-start.2 = (bf16[8,4,16,640]{3,2,1,0:T(8,128)(2,1)}, bf16[8,4,16,640]{3,2,1,0:T(8,128)(2,1)S(1)}, u32[]{:S(2)}) copy-start(bf16[8,4,16,640]{3,2,1,0:T(8,128)(2,1)S(1)} %all-to-all-done.2.tokens_ref) | copy-start | bytes 1966084
  212.3 22.6 %all-to-all-start.1 = ((bf16[8,2,16,1280]{3,2,1,0:T(8,128)(2,1)}), bf16[8,2,16,1280]{3,2,1,0:T(8,128)(2,1)S(1)}, u32[]{:S(2)}, u32[]{:S(2)}) async-start(bf16[8,2,16,1280]{3,2,1,0:T(8,128)(2,1)} %bitcast.46), calls=%async_computation.1 | async-start | bytes 1310720 | tf_op jit(solution)/shard_map/all_to_all | solution.py:332
  (1 other events, 0.8 us)
where the time goes:
time: 260 us; the launch traced here: 259 us
  Pallas kernels  75.1 us (29%)
  blocking collectives  67.7 us (26%)
  waiting for transfers between devices  64.5 us (25%)
  starting transfers between devices  32.8 us (13%)
  local copies, waits for them, and re-layouts  13.4 us (5%)
  other arithmetic  5.17 us (2%)
    all_to_all x1, blocking collectives, on_device(): lax.all_to_all(tokens, 'frame', split_axis=0, concat_axis=0, tiled=True)  45.1 us
    ppermute x3, waiting for transfers between devices, strided_weights(): near = lax.ppermute(mine, 'frame', steps)  35.4 us
    pallas_call x2, Pallas kernels, attention(): pl.pallas_call(attention_kernel, out_shape=jax.ShapeDtypeStruct((frames,...  33.7 us
    ppermute x1, waiting for transfers between devices, on_device(): other = [lax.ppermute(own[0], 'frame', swapped)]  24.9 us
    all_to_all x1, blocking collectives, on_device(): lax.all_to_all(result, 'frame', split_axis=0, concat_axis=0, tiled=True)  22.7 us
    pallas_call x2, Pallas kernels, temporal(): pl.pallas_call(temporal_kernel, out_shape=jax.ShapeDtypeStruct((rows, fra...  22.6 us
    pallas_call x1, Pallas kernels, strided(): pl.pallas_call(functools.partial(strided_kernel, tuple((piece.shape[:2] f...  18.8 us
    all_to_all x1, starting transfers between devices, on_device(): lax.all_to_all(result, 'frame', split_axis=0, concat_axis=0, tiled=True)  5.71 us
  transfers between devices with their start and end apart: 19, of which 6 were waited for; matrix products, arithmetic and copies ran while one was open for 5% of the time, Pallas kernels for 22%

commit v1 on v0

--- a/solution.py
+++ b/solution.py
@@ -48,6 +48,10 @@
                 )
 
 
+def from_row(step, start, columns, channels):
+    return pl.BlockSpec((1, step, columns, channels), lambda r: (0, r + start // step, 0, 0))
+
+
 def temporal(sequence, time_weight, time_bias, start, rows, step):
     _, _, columns, channels = sequence[0].shape
     frames = len(sequence) - 2
@@ -56,8 +60,7 @@
         temporal_kernel,
         out_shape=jax.ShapeDtypeStruct((rows, frames, half, 3 * channels), jnp.bfloat16),
         grid=(rows // step,),
-        in_specs=[pl.BlockSpec((1, step, columns, channels), lambda r: (0, r + start // step, 0, 0))]
-        * len(sequence)
+        in_specs=[from_row(step, start, columns, channels)] * len(sequence)
         + [
             pl.BlockSpec((3 * channels, channels), lambda r: (0, 0)),
             pl.BlockSpec((1, channels), lambda r: (0, 0)),
@@ -72,47 +75,46 @@
     )(*sequence, time_weight.reshape(3 * channels, channels), time_bias.reshape(1, channels))
 
 
-def strided_kernel(spans, where_ref, planes_ref, upper_ref, bias_ref, *refs):
+def strided_kernel(spans, parts, where_ref, upper_ref, bias_ref, *refs):
+    planes_refs, refs = refs[:parts], refs[parts:]
     pieces, (*out_refs, weight, total, sems) = refs[: len(spans)], refs[len(spans) :]
     step = pl.program_id(0)
-    half_rows, _, frames, half_cols, width = planes_ref.shape
+    _, _, frames, half_cols, width = planes_refs[0].shape
+    half_rows = sum(ref.shape[0] for ref in planes_refs)
     count = half_rows * frames * half_cols
     channels = width // 3
     _, units, unit, _ = weight.shape
 
-    def copies():
-        for place, (piece, (taps, run)) in enumerate(zip(pieces, spans)):
-            target = weight.at[pl.ds(where_ref[place, 0], taps), pl.ds(where_ref[place, 1], run)]
-            yield pltpu.make_async_copy(piece, target, sems.at[place])
+    def load(place, piece, run, at):
+        tap = where_ref[place, 0] + at
+        lanes = pl.ds(pl.multiple_of(tap % 3 * channels, LANES), channels)
+        target = weight.at[tap // 3, pl.ds(where_ref[place, 1], run), :, lanes]
+        pltpu.make_async_copy(piece.at[at], target, sems.at[tap // 3]).start()
 
     def product(values, tap):
-        result = None
-        for part in range(3):
-            term = lax.dot_general(
-                values[..., part * channels : (part + 1) * channels].reshape(count, channels),
-                weight[3 * tap + part].reshape(units * unit, channels),
-                (((1,), (1,)), ((), ())),
-                preferred_element_type=jnp.float32,
-            )
-            result = term if result is None else result + term
-        return result
+        pltpu.make_async_copy(weight.at[tap], weight.at[tap], sems.at[tap]).wait()
+        return lax.dot_general(
+            values.reshape(count, width),
+            weight[tap].reshape(units * unit, width),
+            (((1,), (1,)), ((), ())),
+            preferred_element_type=jnp.float32,
+        )
 
     @pl.when(step == 0)
     def _():
-        for copy in copies():
-            copy.start()
-        for copy in copies():
-            copy.wait()
-        values = jnp.concatenate([upper_ref[...], planes_ref[: half_rows - 1, 1]], axis=0)
+        for place, (piece, (taps, run)) in enumerate(zip(pieces, spans)):
+            for at in range(taps):
+                load(place, piece, run, at)
+        values = jnp.concatenate([upper_ref[...]] + [ref[:, 0] for ref in planes_refs], axis=0)[:half_rows]
         total[...] = product(values, 0) + bias_ref[...]
 
     @pl.when(step == 1)
     def _():
-        total[...] += product(planes_ref[:, 0], 1)
+        total[...] += product(jnp.concatenate([ref[:, 0] for ref in planes_refs], axis=0), 2)
 
     @pl.when(step == 2)
     def _():
-        done = total[...] + product(planes_ref[:, 1], 2)
+        done = total[...] + product(jnp.concatenate([ref[:, 0] for ref in planes_refs], axis=0), 1)
         done = done.reshape(half_rows, frames, half_cols, done.shape[1])
         part = half_cols // len(out_refs)
         for chunk, out_ref in enumerate(out_refs):
@@ -120,48 +122,52 @@
 
 
 def strided(planes, upper, pieces, where, bias, chunks):
-    rows, frames, half_cols, width = planes.shape
+    _, frames, half_cols, width = planes[0].shape
     outputs = bias.shape[0]
-    half_rows = rows // 2
+    half_rows = sum(part.shape[0] for part in planes) // 2
     count = half_rows * frames * half_cols
     unit = pieces[0].shape[2]
-    channels = width // 3
     block = (half_rows, frames, half_cols // chunks, outputs)
     anywhere = pl.BlockSpec(memory_space=pl.ANY)
     return pl.pallas_call(
-        functools.partial(strided_kernel, tuple(piece.shape[:2] for piece in pieces)),
+        functools.partial(strided_kernel, tuple(piece.shape[:2] for piece in pieces), len(planes)),
         out_shape=[jax.ShapeDtypeStruct(block, jnp.bfloat16)] * chunks,
         grid=(3,),
         in_specs=[
             pl.BlockSpec(memory_space=pltpu.SMEM),
-            pl.BlockSpec((half_rows, 2, frames, half_cols, width), lambda a: (0, 0, 0, 0, 0)),
             pl.BlockSpec((1, frames, half_cols, width), lambda a: (0, 0, 0, 0)),
             pl.BlockSpec((1, outputs), lambda a: (0, 0)),
+        ]
+        + [
+            pl.BlockSpec(
+                (part.shape[0] // 2, 1, frames, half_cols, width), lambda a: (0, 1 - a // 2, 0, 0, 0)
+            )
+            for part in planes
         ]
         + [anywhere] * len(pieces),
         out_specs=[pl.BlockSpec(block, lambda a: (0, 0, 0, 0))] * chunks,
         scratch_shapes=[
-            pltpu.VMEM((9, outputs // unit, unit, channels), jnp.bfloat16),
+            pltpu.VMEM((3, outputs // unit, unit, width), jnp.bfloat16),
             pltpu.VMEM((count, outputs), jnp.float32),
-            pltpu.SemaphoreType.DMA((len(pieces),)),
+            pltpu.SemaphoreType.DMA((3,)),
         ],
         cost_estimate=pl.CostEstimate(
             flops=6 * count * width * outputs,
-            bytes_accessed=2 * (planes.size + 3 * width * outputs + count * outputs),
+            bytes_accessed=2 * (2 * count * width + 3 * width * outputs + count * outputs),
             transcendentals=0,
         ),
     )(
         where,
-        planes.reshape(half_rows, 2, frames, half_cols, width),
         upper,
         bias.reshape(1, outputs),
+        *(part.reshape(-1, 2, frames, half_cols, width) for part in planes),
         *pieces,
     )
 
 
 def attention_kernel(
     tokens_ref, gain_ref, bias_ref, wq_hbm, wk_hbm, wv_hbm, wo_hbm, out_ref,
-    wq, wk, wv, wo, held, normed, query, key, value, sems,
+    wq, wk, wv, wo, held, normed, query, key, value, scores, weights, sems,
 ):
     copies = []
     for place, (source, target) in enumerate(((wq_hbm, wq), (wk_hbm, wk), (wv_hbm, wv), (wo_hbm, wo))):
@@ -189,42 +195,44 @@
         spread = jnp.mean(centred * centred, axis=-1, keepdims=True)
         result = centred * lax.rsqrt(spread + 1e-05) * gain_ref[...]
         normed[group * rows : (group + 1) * rows, :] = result.astype(jnp.bfloat16)
-    step = 256
     for place, (weight, target) in enumerate(((wq, query), (wk, key), (wv, value))):
         copies[place].wait()
-
-        @pl.loop(0, width // step)
-        def _(n):
-            part = pl.ds(pl.multiple_of(n * step, step), step)
-            target[:, part] = jnp.dot(
-                normed[...], weight[:, part], preferred_element_type=jnp.float32
-            ).astype(jnp.bfloat16)
+        target[...] = jnp.dot(normed[...], weight[...], preferred_element_type=jnp.float32).astype(jnp.bfloat16)
 
     same = (
         lax.broadcasted_iota(jnp.int32, (rows, rows), 0) % 8
         == lax.broadcasted_iota(jnp.int32, (rows, rows), 1) % 8
     )
-
-    @pl.loop(0, groups)
-    def _(group):
-        here = pl.ds(pl.multiple_of(group * rows, rows), rows)
-        sums = [None] * (width // LANES)
-        for head in range(HEADS):
-            low = head * head_width // LANES
-            high = ((head + 1) * head_width - 1) // LANES + 1
+    windows = []
+    for head in range(HEADS):
+        low = head * head_width // LANES
+        high = ((head + 1) * head_width - 1) // LANES + 1
+        lane = lax.broadcasted_iota(jnp.int32, (rows, (high - low) * LANES), 1) + low * LANES
+        mine = (lane >= head * head_width) & (lane < (head + 1) * head_width)
+        windows.append((low, high, mine))
+
+    for group in range(groups):
+        here = slice(group * rows, (group + 1) * rows)
+        for head, (low, high, mine) in enumerate(windows):
             window = slice(low * LANES, high * LANES)
-            lane = lax.broadcasted_iota(jnp.int32, (rows, (high - low) * LANES), 1) + low * LANES
-            mine = (lane >= head * head_width) & (lane < (head + 1) * head_width)
-            zeros = jnp.zeros((rows, (high - low) * LANES), jnp.bfloat16)
-            queries = jnp.where(mine, query[here, window], zeros)
-            scores = lax.dot_general(
+            queries = jnp.where(mine, query[here, window], jnp.zeros(mine.shape, jnp.bfloat16))
+            scores[head] = lax.dot_general(
                 queries, key[here, window], (((1,), (1,)), ((), ())), preferred_element_type=jnp.float32
             )
-            scores = jnp.where(same, scores * scale, MASKED)
-            powers = jnp.exp(scores - jnp.max(scores, axis=-1, keepdims=True))
-            weights = powers * (1.0 / jnp.sum(powers, axis=-1, keepdims=True))
-            values = jnp.where(mine, value[here, window], zeros)
-            part = jnp.dot(weights.astype(jnp.bfloat16), values, preferred_element_type=jnp.float32)
+
+        @pl.loop(0, HEADS // 4)
+        def _(quarter):
+            part = pl.ds(quarter * 4, 4)
+            some = jnp.where(same[None], scores[part] * scale, MASKED)
+            powers = jnp.exp(some - jnp.max(some, axis=-1, keepdims=True))
+            share_of = 1.0 / jnp.sum(powers, axis=-1, keepdims=True)
+            weights[part] = (powers * share_of).astype(jnp.bfloat16)
+
+        sums = [None] * (width // LANES)
+        for head, (low, high, mine) in enumerate(windows):
+            window = slice(low * LANES, high * LANES)
+            values = jnp.where(mine, value[here, window], jnp.zeros(mine.shape, jnp.bfloat16))
+            part = jnp.dot(weights[head], values, preferred_element_type=jnp.float32)
             for block in range(low, high):
                 piece = part[:, (block - low) * LANES : (block - low + 1) * LANES]
                 sums[block] = piece if sums[block] is None else sums[block] + piece
@@ -232,16 +240,11 @@
             normed[here, block * LANES : (block + 1) * LANES] = total.astype(jnp.bfloat16)
 
     copies[3].wait()
-
-    @pl.loop(0, width // step)
-    def _(n):
-        part = pl.ds(pl.multiple_of(n * step, step), step)
-        output = jnp.dot(normed[...], wo[:, part], preferred_element_type=jnp.float32)
-        output = output + bias_ref[:, part]
-        for group in range(groups):
-            here = slice(group * rows, (group + 1) * rows)
-            piece = (output[here] + held[here, part].astype(jnp.float32)).reshape(frames, 8, step)
-            out_ref[:, group * 8 : group * 8 + 8, part] = piece.astype(jnp.bfloat16)
+    output = jnp.dot(normed[...], wo[...], preferred_element_type=jnp.float32)
+    output = output + bias_ref[...] + held[...].astype(jnp.float32)
+    for group in range(groups):
+        piece = output[group * rows : (group + 1) * rows].reshape(frames, 8, width)
+        out_ref[:, group * 8 : group * 8 + 8, :] = piece.astype(jnp.bfloat16)
 
 
 def attention(tokens, norm_gain, out_bias, w_query, w_key, w_value, w_out):
@@ -257,7 +260,13 @@
         out_shape=jax.ShapeDtypeStruct((frames, pixels, width), jnp.bfloat16),
         in_specs=[inside, inside, inside, anywhere, anywhere, anywhere, anywhere],
         out_specs=inside,
-        scratch_shapes=[weight] * 4 + [rows] * 5 + [pltpu.SemaphoreType.DMA((4,))],
+        scratch_shapes=[weight] * 4
+        + [rows] * 5
+        + [
+            pltpu.VMEM((HEADS, frames * 8, frames * 8), jnp.float32),
+            pltpu.VMEM((HEADS, frames * 8, frames * 8), jnp.bfloat16),
+            pltpu.SemaphoreType.DMA((4,)),
+        ],
         cost_estimate=pl.CostEstimate(
             flops=8 * count * width * width,
             bytes_accessed=8 * width * width + 4 * count * width,
@@ -289,45 +298,55 @@
 
     everyone = range(groups)
     swapped = [(at, at ^ 1) for at in everyone]
-    own = [
-        lax.dynamic_slice_in_dim(features, jnp.where(side == 0, at, frames_here - 1 - at), 1, axis=0)
-        for at in range(frames_here)
-    ]
-    other = [lax.ppermute(own[0], "frame", swapped)]
-    later = list(own[1:])
-    other[0], *later = lax.optimization_barrier([other[0]] + later)
-    other += [lax.ppermute(value, "frame", swapped) for value in later]
     outward = [(at, at + (2 if at % 2 else -2)) for at in everyone]
     inward = [(at, at + (-2 if at % 2 else 2)) for at in everyone]
     inside = lambda pairs: [(source, target) for source, target in pairs if 0 <= target < groups]
-    last = lax.ppermute(own[0], "frame", inside(outward))
-    first = lax.ppermute(other[0], "frame", inside(inward))
-    sequence = [first] + own + other[::-1] + [last]
+    half = rows_here // 2
+    starts = (half, 0)
+
+    def own_frame(at, start):
+        place = jnp.where(side == 0, at, frames_here - 1 - at)
+        return lax.dynamic_slice(features, (place, start, 0, 0), (1, half, columns, channels))
+
+    def moved_along(value, pairs):
+        return lax.ppermute(value, "frame", pairs)
+
+    own = [[own_frame(at, start) for at in range(frames_here)] for start in starts]
+    outer = [moved_along(value[0], swapped) for value in own]
+    last = [moved_along(value[0], inside(outward)) for value in own]
+    first = [moved_along(value, inside(inward)) for value in outer]
+    inner = [[moved_along(each, swapped) for each in value[1:]] for value in own]
+    sequences = [
+        [first[part]] + own[part] + inner[part][::-1] + [outer[part], last[part]] for part in range(len(starts))
+    ]
 
     pieces, where, distant = strided_weights(down_weight, frame, row, channels)
 
     taps = jnp.where(side == 0, time_weight, time_weight[::-1])
-    final = temporal(sequence, taps, time_bias, rows_here - 1, 1, 1)
+    final = temporal(sequences[0], taps, time_bias, half - 1, 1, 1)
     upper = passed_along(final, "row", 1)
-    planes = temporal(sequence, taps, time_bias, 0, rows_here, 2)
+    lower_planes = temporal(sequences[0], taps, time_bias, 0, half, 2)
+    upper_planes = temporal(sequences[1], taps, time_bias, 0, half, 2)
+    lower_planes, *distant = lax.optimization_barrier([lower_planes] + distant)
+    planes = [upper_planes, lower_planes]
     shares = down_bias.reshape(lines, 2, down_bias.shape[0] // groups)
     bias = lax.dynamic_index_in_dim(shares, side, axis=1, keepdims=False).reshape(-1)
-    planes, *distant = lax.optimization_barrier([planes] + distant)
     pieces += [lax.ppermute(value, "row", [(at, at ^ 1) for at in range(lax.axis_size("row"))]) for value in distant]
 
     half_rows, half_cols = rows_here // 2, columns // 2
     pixels_here = half_rows * half_cols // groups
     chunks = 2 if groups == half_rows and pixels_here % 16 == 0 else 1
-    results = []
+    moved, results = [], []
+    part = pixels_here // chunks
     for coarse in strided(planes, upper, pieces, where, bias, chunks):
         half_width = coarse.shape[-1]
-        part = pixels_here // chunks
         tokens = coarse
         if groups != half_rows:
             tokens = tokens.transpose(1, 0, 2, 3).reshape(2 * frames_here, groups, part, half_width)
             tokens = tokens.transpose(1, 0, 2, 3)
-        moved = lax.all_to_all(tokens, "frame", split_axis=0, concat_axis=0, tiled=True)
-        result = attention(moved, norm_gain, out_bias, w_query, w_key, w_value, w_out)
+        moved.append(lax.all_to_all(tokens, "frame", split_axis=0, concat_axis=0, tiled=True))
+    for tokens in moved:
+        result = attention(tokens, norm_gain, out_bias, w_query, w_key, w_value, w_out)
         result = result.reshape(groups, frames_here, part, 2 * half_width)
         results.append(lax.all_to_all(result, "frame", split_axis=0, concat_axis=0, tiled=True))
     returned = jnp.concatenate(results, axis=2).transpose(1, 0, 2, 3)

time: 260 us -> 226 us (0.87)
  waiting for transfers between devices: 64.5 us -> 36.3 us
  blocking collectives: 67.7 us -> 45.9 us
  starting transfers between devices: 32.8 us -> 54.5 us
  Pallas kernels: 75.1 us -> 66.2 us
  local copies, waits for them, and re-layouts: 13.4 us -> 17 us
    ppermute x4 -> x8, starting transfers between devices: 9.1 us -> 32.7 us  [moved_along(): return lax.ppermute(value, 'frame', pairs)]
    ppermute x4 -> x8, waiting for transfers between devices: 24.9 us -> 2.27 us  [moved_along(): return lax.ppermute(value, 'frame', pairs)]
    all_to_all x1, blocking collectives: 45.1 us -> 24.4 us  [on_device(): lax.all_to_all(tokens, 'frame', split_axis=0, concat_axis=0, tiled=True)]
    ppermute x3, waiting for transfers between devices: 35.4 us -> 24.2 us  [strided_weights(): near = lax.ppermute(mine, 'frame', steps)]
    pallas_call x2, Pallas kernels: 33.7 us -> 23.1 us  [attention(): pl.pallas_call(attention_kernel, out_shape=jax.ShapeDtypeStruct((frames,...]
    all_to_all x1, waiting for transfers between devices: 0.01 us -> 5.93 us  [on_device(): lax.all_to_all(result, 'frame', split_axis=0, concat_axis=0, tiled=True)]
    all_to_all x1, waiting for transfers between devices: 0.01 us -> 3.88 us  [on_device(): lax.all_to_all(tokens, 'frame', split_axis=0, concat_axis=0, tiled=True)]
    ppermute x3, waiting for transfers between devices: 3.41 us -> 0.01 us  [strided_weights(): far = lax.ppermute(sent, 'row', [(at, at ^ 2) for at in rows])]
  transfers between devices with their start and end apart: 19 -> 23, of which waited for: 6 -> 5; matrix products, arithmetic and copies ran while one was open for 5% -> 8% of each run, Pallas kernels for 22% -> 22%
where the time goes in v1:
time: 226 us; the launch traced here: 225 us
  Pallas kernels  66.2 us (29%)
  starting transfers between devices  54.5 us (24%)
  blocking collectives  45.9 us (20%)
  waiting for transfers between devices  36.3 us (16%)
  local copies, waits for them, and re-layouts  17 us (8%)
  other arithmetic  5.24 us (2%)
    ppermute x8, starting transfers between devices, moved_along(): return lax.ppermute(value, 'frame', pairs)  32.7 us
    pallas_call x3, Pallas kernels, temporal(): pl.pallas_call(temporal_kernel, out_shape=jax.ShapeDtypeStruct((rows, fra...  25.7 us
    all_to_all x1, blocking collectives, on_device(): lax.all_to_all(tokens, 'frame', split_axis=0, concat_axis=0, tiled=True)  24.4 us
    ppermute x3, waiting for transfers between devices, strided_weights(): near = lax.ppermute(mine, 'frame', steps)  24.2 us
    pallas_call x2, Pallas kernels, attention(): pl.pallas_call(attention_kernel, out_shape=jax.ShapeDtypeStruct((frames,...  23.1 us
    all_to_all x1, blocking collectives, on_device(): lax.all_to_all(result, 'frame', split_axis=0, concat_axis=0, tiled=True)  21.5 us
    pallas_call x1, Pallas kernels, strided(): pl.pallas_call(functools.partial(strided_kernel, tuple((piece.shape[:2] f...  17.4 us
    all_to_all x1, waiting for transfers between devices, on_device(): lax.all_to_all(result, 'frame', split_axis=0, concat_axis=0, tiled=True)  5.93 us
  transfers between devices with their start and end apart: 23, of which 5 were waited for; matrix products, arithmetic and copies ran while one was open for 8% of the time, Pallas kernels for 22%

profile of v1, /device:TPU:0, one launch (start us, length us, event | category | flops | bytes accessed | tf_op | source)
XLA Modules:
  0.0 225.4 jit_solution(1261125205686992340)
XLA Ops:
  0.0 1.9 constant_dynamic-slice_fusion.3
  1.9 3.1 %collective-permute-start.9 = (bf16[5,1,80,640]{3,2,1,0:T(8,128)(2,1)}, bf16[5,1,80,640]{3,2,1,0:T(8,128)(2,1)}, u32[]{:S(2)}, u32[]{:S(2)}) collective-permute-start(bf16[5,1,80,640]{3,2,1,0:T(8,128)(2,1)} %constant_dynamic-slice_fusion.3), channel_id=1, source_target_pairs={{0,8},{4,12},{8,0},{12,4},{16,24},{20,28},{24,16},{28,20},{1,9},{5... | collective-permute-start | bytes 1536008 | tf_op jit(solution)/shard_map/ppermute | solution.py:375
  4.9 2.6 %collective-permute-start.11 = (bf16[5,1,80,640]{3,2,1,0:T(8,128)(2,1)}, bf16[5,1,80,640]{3,2,1,0:T(8,128)(2,1)}, u32[]{:S(2)}, u32[]{:S(2)}) collective-permute-start(bf16[5,1,80,640]{3,2,1,0:T(8,128)(2,1)} %constant_dynamic-slice_fusion.3), channel_id=1, source_target_pairs={{0,16},{4,20},{8,24},{12,28},{16,0},{20,4},{24,8},{28,12},{1,17},{... | collective-permute-start | bytes 1536008 | tf_op jit(solution)/shard_map/ppermute | solution.py:375
  7.5 3.0 %constant_dynamic-slice_fusion.4 = (bf16[1,8,64,640]{3,2,1,0:T(8,128)(2,1)}, bf16[1,8,64,640]{3,2,1,0:T(8,128)(2,1)S(1)}, bf16[1,8,64,640]{3,2,1,0:T(8,128)(2,1)S(1)}, bf16[1,8,64,640]{3,2,1,0:T(8,128)(2,1)}) fusion(bf16[2,16,64,640]{3,2,1,0:T(8,128)(2,1)} %param.11, s32[]{:T(128)S(6)} %select_n.64, s32[]{:T(128)S(6)} %select_n.63), kind=kLoop, calls=%fused_computation.7 | loop fusion | bytes 5242888 | tf_op jit(solution)/shard_map/dynamic_slice | solution.py:309
  10.6 1.7 collective-permute-start
  12.6 4.6 %reverse_select_fusion = bf16[3,640,640]{2,1,0:T(8,128)(2,1)} fusion(bf16[3,640,640]{2,1,0:T(8,128)(2,1)} %param.12, pred[]{:T(512)S(6)} %eq.6), kind=kLoop, calls=%fused_computation | loop fusion | flops 1228800 | bytes 4915201 | tf_op jit(solution)/shard_map/jit(_where)/select_n | solution.py:325
  17.2 9.9 %collective-permute-done.9.refs_3_ = bf16[5,1,80,640]{3,2,1,0:T(8,128)(2,1)} collective-permute-done((bf16[5,1,80,640]{3,2,1,0:T(8,128)(2,1)}, bf16[5,1,80,640]{3,2,1,0:T(8,128)(2,1)}, u32[]{:S(2)}, u32[]{:S(2)}) %collective-permute-start.9) | collective-permute-done | bytes 512032 | tf_op jit(solution)/shard_map/ppermute | solution.py:375
  28.4 14.2 %collective-permute-done.11.refs_6_ = bf16[5,1,80,640]{3,2,1,0:T(8,128)(2,1)} collective-permute-done((bf16[5,1,80,640]{3,2,1,0:T(8,128)(2,1)}, bf16[5,1,80,640]{3,2,1,0:T(8,128)(2,1)}, u32[]{:S(2)}, u32[]{:S(2)}) %collective-permute-start.11) | collective-permute-done | bytes 512032 | tf_op jit(solution)/shard_map/ppermute | solution.py:375
  42.7 1.5 collective-permute-start.5
  44.9 1.3 collective-permute-start.8
  46.2 1.8 constant_dynamic-slice_fusion.2
  48.0 12.7 %collective-permute-start.1 = (bf16[1,8,64,640]{3,2,1,0:T(8,128)(2,1)S(1)}, bf16[1,8,64,640]{3,2,1,0:T(8,128)(2,1)S(1)}, u32[]{:S(2)}, u32[]{:S(2)}) collective-permute-start(bf16[1,8,64,640]{3,2,1,0:T(8,128)(2,1)S(1)} %collective-permute-done.refs_4_), channel_id=1, source_target_pairs={{0,8},{8,16},{12,4},{16,24},{20,12},{28,20},{1,9},{9,17},{13,5},{1... | collective-permute-start | bytes 1966088 | tf_op jit(solution)/shard_map/ppermute | solution.py:312
  60.7 1.8 constant_dynamic-slice_fusion.1
  62.6 1.8 constant_dynamic-slice_fusion
  64.3 1.5 collective-permute-start.10
  66.4 2.2 collective-permute-done.7.refs_3_
  68.6 1.5 collective-permute-start.14
  70.3 13.4 %collective-permute-start.6 = (bf16[1,8,64,640]{3,2,1,0:T(8,128)(2,1)}, bf16[1,8,64,640]{3,2,1,0:T(8,128)(2,1)}, u32[]{:S(2)}, u32[]{:S(2)}) collective-permute-start(bf16[1,8,64,640]{3,2,1,0:T(8,128)(2,1)} %copy-done.12), channel_id=1, source_target_pairs={{0,8},{8,16},{12,4},{16,24},{20,12},{28,20},{1,9},{9,17},{13,5},{1... | collective-permute-start | bytes 1966088 | tf_op jit(solution)/shard_map/ppermute | solution.py:312
  87.4 3.8 %shard_map.109 = bf16[1,4,32,1920]{3,2,1,0:T(8,128)(2,1)} custom-call(bf16[1,8,64,640]{3,2,1,0:T(8,128)(2,1)} %copy-done.6, bf16[1,8,64,640]{3,2,1,0:T(8,128)(2,1)} %copy-done.2, bf16[1,8,64,640]{3,2,1,0:T(8,128)(2,1)} %copy-done.1, bf16[1,8,64,640]{3,2,1,0:T(8,128)(2,1)} %copy-done.4, bf16[1,8,64,640]{3,2,1,0:T(8,128)(2,1)} %copy-done.3, ...), custom_call_target="tpu_custom_call" | custom-call | flops 629145600 | bytes 1802240 | tf_op jit(solution)/shard_map/pallas_call | solution.py:59
  91.7 2.1 collective-permute-start.4
  93.8 11.0 %shard_map.111 = bf16[8,4,32,1920]{3,2,1,0:T(8,128)(2,1)} custom-call(bf16[1,8,64,640]{3,2,1,0:T(8,128)(2,1)} %copy-done.6, bf16[1,8,64,640]{3,2,1,0:T(8,128)(2,1)} %copy-done.2, bf16[1,8,64,640]{3,2,1,0:T(8,128)(2,1)} %copy-done.1, bf16[1,8,64,640]{3,2,1,0:T(8,128)(2,1)} %copy-done.4, bf16[1,8,64,640]{3,2,1,0:T(8,128)(2,1)} %copy-done.3, ...), custom_call_target="tpu_custom_call" | custom-call | flops 5033164800 | bytes 14417920 | tf_op jit(solution)/shard_map/pallas_call | solution.py:59
  104.8 1.6 collective-permute-start.18
  106.9 11.0 %shard_map.110 = bf16[8,4,32,1920]{3,2,1,0:T(8,128)(2,1)} custom-call(bf16[1,8,64,640]{3,2,1,0:T(8,128)(2,1)} %collective-permute-done.6.refs_0_, bf16[1,8,64,640]{3,2,1,0:T(8,128)(2,1)} %get-tuple-element.20.refs_1_, bf16[1,8,64,640]{3,2,1,0:T(8,128)(2,1)} %get-tuple-element.17.refs_2_, bf16[1,8,64,640]{3,2,1,0:T(8,128)(2,1)} %copy-done.13, ...), custom_call_target="tpu_custom_call" | custom-call | flops 5033164800 | bytes 14417920 | tf_op jit(solution)/shard_map/pallas_call | solution.py:59
  119.3 17.4 %shard_map.112 = (bf16[8,4,16,640]{3,2,1,0:T(8,128)(2,1)}, bf16[8,4,16,640]{3,2,1,0:T(8,128)(2,1)}) custom-call(s32[13,2]{1,0:T(8,128)} %stack.159.where_ref, bf16[1,4,32,1920]{3,2,1,0:T(8,128)(2,1)} %copy-done.16, f32[1,640]{1,0:T(1,128)} %reshape_reshape.6.bias_ref, bf16[4,2,4,32,1920]{4,3,2,1,0:T(8,128)(2,1)} %bitcast.53, ...), custom_call_target="tpu_custom_call" | custom-call | flops 7549747200 | bytes 16547840 | tf_op jit(solution)/shard_map/pallas_call | solution.py:132
  136.7 24.4 %all_to_all.20.tokens_ref = bf16[8,4,16,640]{3,2,1,0:T(8,128)(2,1)} all-to-all(bf16[8,4,16,640]{3,2,1,0:T(8,128)(2,1)} %get-tuple-element.16), channel_id=1, replica_groups=mesh['frame'=8,'row'=4] {'frame'}, dimensions={0} | all-to-all | bytes 1310720 | tf_op jit(solution)/shard_map/all_to_all | solution.py:347
  161.1 3.8 %all-to-all-start = ((bf16[8,4,16,640]{3,2,1,0:T(8,128)(2,1)}), bf16[8,4,16,640]{3,2,1,0:T(8,128)(2,1)S(1)}, u32[]{:S(2)}, u32[]{:S(2)}) async-start(bf16[8,4,16,640]{3,2,1,0:T(8,128)(2,1)} %get-tuple-element.15), calls=%async_computation | async-start | bytes 1310720 | tf_op jit(solution)/shard_map/all_to_all | solution.py:347
  166.1 11.5 %shard_map.114 = bf16[16,16,1280]{2,1,0:T(8,128)(2,1)} custom-call(bf16[8,4,16,640]{3,2,1,0:T(8,128)(2,1)} %all_to_all.20.tokens_ref, f32[1,1280]{1,0:T(1,128)} %reshape.39.gain_ref, f32[1,1280]{1,0:T(1,128)} %reshape.40.bias_ref, bf16[1280,1280]{1,0:T(8,128)(2,1)} %wq_hbm.3, bf16[1280,1280]{1,0:T(8,128)(2,1)} %wk_hbm.3, bf16[1280,1280]{1,0:T(8,128)(2,1)} %wv_hbm.3, ...), custom_call_target="tpu_custom_call" | custom-call | flops 3355443200 | bytes 14417920 | tf_op jit(solution)/shard_map/pallas_call | solution.py:258
  177.6 3.9 %all-to-all-done.tokens_ref = bf16[8,4,16,640]{3,2,1,0:T(8,128)(2,1)S(1)} async-done(((bf16[8,4,16,640]{3,2,1,0:T(8,128)(2,1)}), bf16[8,4,16,640]{3,2,1,0:T(8,128)(2,1)S(1)}, u32[]{:S(2)}, u32[]{:S(2)}) %all-to-all-start) | async-done | bytes 655392 | tf_op jit(solution)/shard_map/all_to_all | solution.py:347
  181.5 3.6 %all-to-all-start.3 = ((bf16[8,2,16,1280]{3,2,1,0:T(8,128)(2,1)}), bf16[8,2,16,1280]{3,2,1,0:T(8,128)(2,1)S(1)}, u32[]{:S(2)}, u32[]{:S(2)}) async-start(bf16[8,2,16,1280]{3,2,1,0:T(8,128)(2,1)} %bitcast.48), calls=%async_computation.3 | async-start | bytes 1310720 | tf_op jit(solution)/shard_map/all_to_all | solution.py:351
  185.1 11.5 %shard_map.113 = bf16[16,16,1280]{2,1,0:T(8,128)(2,1)} custom-call(bf16[8,4,16,640]{3,2,1,0:T(8,128)(2,1)} %copy-done, f32[1,1280]{1,0:T(1,128)} %reshape.39.gain_ref, f32[1,1280]{1,0:T(1,128)} %reshape.40.bias_ref, bf16[1280,1280]{1,0:T(8,128)(2,1)} %wq_hbm.3, bf16[1280,1280]{1,0:T(8,128)(2,1)} %wk_hbm.3, bf16[1280,1280]{1,0:T(8,128)(2,1)} %wv_hbm.3, ...), custom_call_target="tpu_custom_call" | custom-call | flops 3355443200 | bytes 14417920 | tf_op jit(solution)/shard_map/pallas_call | solution.py:258
  196.7 5.9 %all-to-all-done.3 = bf16[8,2,16,1280]{3,2,1,0:T(8,128)(2,1)S(1)} async-done(((bf16[8,2,16,1280]{3,2,1,0:T(8,128)(2,1)}), bf16[8,2,16,1280]{3,2,1,0:T(8,128)(2,1)S(1)}, u32[]{:S(2)}, u32[]{:S(2)}) %all-to-all-start.3) | async-done | bytes 655392 | tf_op jit(solution)/shard_map/all_to_all | solution.py:351
  202.6 21.5 %all_to_all.21 = bf16[8,2,16,1280]{3,2,1,0:T(8,128)(2,1)S(1)} all-to-all(bf16[8,2,16,1280]{3,2,1,0:T(8,128)(2,1)} %bitcast.49), channel_id=1, replica_groups=mesh['frame'=8,'row'=4] {'frame'}, dimensions={0} | all-to-all | bytes 1310720 | tf_op jit(solution)/shard_map/all_to_all | solution.py:351
  (84 shorter events, 11.5 us)
Async XLA Ops:
  1.9 25.3 %collective-permute-start.9 = (bf16[5,1,80,640]{3,2,1,0:T(8,128)(2,1)}, bf16[5,1,80,640]{3,2,1,0:T(8,128)(2,1)}, u32[]{:S(2)}, u32[]{:S(2)}) collective-permute-start(bf16[5,1,80,640]{3,2,1,0:T(8,128)(2,1)} %constant_dynamic-slice_fusion.3), channel_id=1, source_target_pairs={{0,8},{4,12},{8,0},{12,4},{16,24},{20,28},{24,16},{28,20},{1,9},{5... | collective-permute-start | bytes 1536008 | tf_op jit(solution)/shard_map/ppermute | solution.py:375
  4.9 37.7 %collective-permute-start.11 = (bf16[5,1,80,640]{3,2,1,0:T(8,128)(2,1)}, bf16[5,1,80,640]{3,2,1,0:T(8,128)(2,1)}, u32[]{:S(2)}, u32[]{:S(2)}) collective-permute-start(bf16[5,1,80,640]{3,2,1,0:T(8,128)(2,1)} %constant_dynamic-slice_fusion.3), channel_id=1, source_target_pairs={{0,16},{4,20},{8,24},{12,28},{16,0},{20,4},{24,8},{28,12},{1,17},{... | collective-permute-start | bytes 1536008 | tf_op jit(solution)/shard_map/ppermute | solution.py:375
  7.5 36.6 %collective-permute-start.13 = (bf16[5,1,80,640]{3,2,1,0:T(8,128)(2,1)}, bf16[5,1,80,640]{3,2,1,0:T(8,128)(2,1)}, u32[]{:S(2)}, u32[]{:S(2)}) collective-permute-start(bf16[5,1,80,640]{3,2,1,0:T(8,128)(2,1)} %constant_dynamic-slice_fusion.3), channel_id=1, source_target_pairs={{0,24},{4,28},{8,16},{12,20},{16,8},{20,12},{24,0},{28,4},{1,25},{... | collective-permute-start | bytes 1536008 | tf_op jit(solution)/shard_map/ppermute | solution.py:375
  10.6 16.6 %copy-start.2 = (bf16[1,8,64,640]{3,2,1,0:T(8,128)(2,1)}, bf16[1,8,64,640]{3,2,1,0:T(8,128)(2,1)S(1)}, u32[]{:S(2)}) copy-start(bf16[1,8,64,640]{3,2,1,0:T(8,128)(2,1)S(1)} %get-tuple-element.19.refs_1_) | copy-start | bytes 1966084
  10.6 34.3 %collective-permute-start = (bf16[1,8,64,640]{3,2,1,0:T(8,128)(2,1)S(1)}, bf16[1,8,64,640]{3,2,1,0:T(8,128)(2,1)S(1)}, u32[]{:S(2)}, u32[]{:S(2)}) collective-permute-start(bf16[1,8,64,640]{3,2,1,0:T(8,128)(2,1)S(1)} %get-tuple-element.19.refs_1_), channel_id=1, source_target_pairs={{0,4},{4,0},{8,12},{12,8},{16,20},{20,16},{24,28},{28,24},{1,5},{5... | collective-permute-start | bytes 1966088 | tf_op jit(solution)/shard_map/ppermute | solution.py:312
  12.3 35.7 %collective-permute-start.2 = (bf16[1,8,64,640]{3,2,1,0:T(8,128)(2,1)S(1)}, bf16[1,8,64,640]{3,2,1,0:T(8,128)(2,1)S(1)}, u32[]{:S(2)}, u32[]{:S(2)}) collective-permute-start(bf16[1,8,64,640]{3,2,1,0:T(8,128)(2,1)S(1)} %get-tuple-element.18.refs_2_), channel_id=1, source_target_pairs={{0,4},{4,0},{8,12},{12,8},{16,20},{20,16},{24,28},{28,24},{1,5},{5... | collective-permute-start | bytes 1966088 | tf_op jit(solution)/shard_map/ppermute | solution.py:312
  12.6 31.6 %copy-start.7 = (bf16[1,8,64,640]{3,2,1,0:T(8,128)(2,1)S(1)}, bf16[1,8,64,640]{3,2,1,0:T(8,128)(2,1)}, u32[]{:S(2)}) copy-start(bf16[1,8,64,640]{3,2,1,0:T(8,128)(2,1)} %get-tuple-element.17.refs_2_) | copy-start | bytes 1966084
  17.2 66.6 %copy-start.11 = (f32[640]{0:T(1024)S(1)}, f32[640]{0:T(1024)}, u32[]{:S(2)}) copy-start(f32[640]{0:T(1024)} %param.13) | copy-start | bytes 7684
  17.2 67.2 %copy-start.8 = (f32[1280]{0:T(1024)S(1)}, f32[1280]{0:T(1024)}, u32[]{:S(2)}) copy-start(f32[1280]{0:T(1024)} %param.15) | copy-start | bytes 15364
  27.1 37.2 %collective-permute-start.3 = (bf16[1,8,64,640]{3,2,1,0:T(8,128)(2,1)S(1)}, bf16[1,8,64,640]{3,2,1,0:T(8,128)(2,1)S(1)}, u32[]{:S(2)}, u32[]{:S(2)}) collective-permute-start(bf16[1,8,64,640]{3,2,1,0:T(8,128)(2,1)S(1)} %get-tuple-element.19.refs_1_), channel_id=1, source_target_pairs={{4,12},{8,0},{12,20},{16,8},{20,28},{24,16},{5,13},{9,1},{13,21},{... | collective-permute-start | bytes 1966088 | tf_op jit(solution)/shard_map/ppermute | solution.py:312
  42.7 23.2 %collective-permute-start.5 = (bf16[1,8,64,640]{3,2,1,0:T(8,128)(2,1)}, bf16[1,8,64,640]{3,2,1,0:T(8,128)(2,1)S(1)}, u32[]{:S(2)}, u32[]{:S(2)}) collective-permute-start(bf16[1,8,64,640]{3,2,1,0:T(8,128)(2,1)} %get-tuple-element.20.refs_1_), channel_id=1, source_target_pairs={{0,4},{4,0},{8,12},{12,8},{16,20},{20,16},{24,28},{28,24},{1,5},{5... | collective-permute-start | bytes 1966088 | tf_op jit(solution)/shard_map/ppermute | solution.py:312
  44.2 24.5 %collective-permute-start.7 = (bf16[1,8,64,640]{3,2,1,0:T(8,128)(2,1)S(1)}, bf16[1,8,64,640]{3,2,1,0:T(8,128)(2,1)S(1)}, u32[]{:S(2)}, u32[]{:S(2)}) collective-permute-start(bf16[1,8,64,640]{3,2,1,0:T(8,128)(2,1)S(1)} %copy-done.7), channel_id=1, source_target_pairs={{0,4},{4,0},{8,12},{12,8},{16,20},{20,16},{24,28},{28,24},{1,5},{5... | collective-permute-start | bytes 1966088 | tf_op jit(solution)/shard_map/ppermute | solution.py:312
  44.9 42.1 %copy-start.3 = (bf16[1,8,64,640]{3,2,1,0:T(8,128)(2,1)}, bf16[1,8,64,640]{3,2,1,0:T(8,128)(2,1)S(1)}, u32[]{:S(2)}) copy-start(bf16[1,8,64,640]{3,2,1,0:T(8,128)(2,1)S(1)} %collective-permute-done.refs_4_) | copy-start | bytes 1966084
  44.9 25.4 %collective-permute-start.8 = (bf16[1,8,64,640]{3,2,1,0:T(8,128)(2,1)}, bf16[1,8,64,640]{3,2,1,0:T(8,128)(2,1)}, u32[]{:S(2)}, u32[]{:S(2)}) collective-permute-start(bf16[1,8,64,640]{3,2,1,0:T(8,128)(2,1)} %get-tuple-element.20.refs_1_), channel_id=1, source_target_pairs={{4,12},{8,0},{12,20},{16,8},{20,28},{24,16},{5,13},{9,1},{13,21},{... | collective-permute-start | bytes 1966088 | tf_op jit(solution)/shard_map/ppermute | solution.py:312
  48.0 38.9 %copy-start.4 = (bf16[1,8,64,640]{3,2,1,0:T(8,128)(2,1)}, bf16[1,8,64,640]{3,2,1,0:T(8,128)(2,1)S(1)}, u32[]{:S(2)}) copy-start(bf16[1,8,64,640]{3,2,1,0:T(8,128)(2,1)S(1)} %collective-permute-done.2.refs_3_) | copy-start | bytes 1966084
  48.0 38.4 %collective-permute-start.1 = (bf16[1,8,64,640]{3,2,1,0:T(8,128)(2,1)S(1)}, bf16[1,8,64,640]{3,2,1,0:T(8,128)(2,1)S(1)}, u32[]{:S(2)}, u32[]{:S(2)}) collective-permute-start(bf16[1,8,64,640]{3,2,1,0:T(8,128)(2,1)S(1)} %collective-permute-done.refs_4_), channel_id=1, source_target_pairs={{0,8},{8,16},{12,4},{16,24},{20,12},{28,20},{1,9},{9,17},{13,5},{1... | collective-permute-start | bytes 1966088 | tf_op jit(solution)/shard_map/ppermute | solution.py:312
  64.3 22.6 %copy-start.5 = (bf16[1,8,64,640]{3,2,1,0:T(8,128)(2,1)}, bf16[1,8,64,640]{3,2,1,0:T(8,128)(2,1)S(1)}, u32[]{:S(2)}) copy-start(bf16[1,8,64,640]{3,2,1,0:T(8,128)(2,1)S(1)} %collective-permute-done.3.refs_5_) | copy-start | bytes 1966084
  64.3 22.1 %collective-permute-start.10 = (bf16[4,1,80,640]{3,2,1,0:T(8,128)(2,1)}, bf16[4,1,80,640]{3,2,1,0:T(8,128)(2,1)}, u32[]{:S(2)}, u32[]{:S(2)}) collective-permute-start(bf16[4,1,80,640]{3,2,1,0:T(8,128)(2,1)} %constant_dynamic-slice_fusion.2), channel_id=1, source_target_pairs={{0,2},{1,3},{2,0},{3,1},{4,6},{5,7},{6,4},{7,5},{8,10},{9,11},{10,... | collective-permute-start | bytes 1228808 | tf_op jit(solution)/shard_map/ppermute | solution.py:377
  65.8 25.3 %collective-permute-start.12 = (bf16[4,1,80,640]{3,2,1,0:T(8,128)(2,1)}, bf16[4,1,80,640]{3,2,1,0:T(8,128)(2,1)}, u32[]{:S(2)}, u32[]{:S(2)}) collective-permute-start(bf16[4,1,80,640]{3,2,1,0:T(8,128)(2,1)} %constant_dynamic-slice_fusion.1), channel_id=1, source_target_pairs={{0,2},{1,3},{2,0},{3,1},{4,6},{5,7},{6,4},{7,5},{8,10},{9,11},{10,... | collective-permute-start | bytes 1228808 | tf_op jit(solution)/shard_map/ppermute | solution.py:377
  68.6 23.0 %collective-permute-start.14 = (bf16[4,1,80,640]{3,2,1,0:T(8,128)(2,1)}, bf16[4,1,80,640]{3,2,1,0:T(8,128)(2,1)}, u32[]{:S(2)}, u32[]{:S(2)}) collective-permute-start(bf16[4,1,80,640]{3,2,1,0:T(8,128)(2,1)} %constant_dynamic-slice_fusion), channel_id=1, source_target_pairs={{0,2},{1,3},{2,0},{3,1},{4,6},{5,7},{6,4},{7,5},{8,10},{9,11},{10,... | collective-permute-start | bytes 1228808 | tf_op jit(solution)/shard_map/ppermute | solution.py:377
  70.3 36.2 %collective-permute-start.6 = (bf16[1,8,64,640]{3,2,1,0:T(8,128)(2,1)}, bf16[1,8,64,640]{3,2,1,0:T(8,128)(2,1)}, u32[]{:S(2)}, u32[]{:S(2)}) collective-permute-start(bf16[1,8,64,640]{3,2,1,0:T(8,128)(2,1)} %copy-done.12), channel_id=1, source_target_pairs={{0,8},{8,16},{12,4},{16,24},{20,12},{28,20},{1,9},{9,17},{13,5},{1... | collective-permute-start | bytes 1966088 | tf_op jit(solution)/shard_map/ppermute | solution.py:312
  86.4 18.3 %collective-permute-start.15 = (bf16[5,1,80,640]{3,2,1,0:T(8,128)(2,1)}, bf16[5,1,80,640]{3,2,1,0:T(8,128)(2,1)S(1)}, u32[]{:S(2)}, u32[]{:S(2)}) collective-permute-start(bf16[5,1,80,640]{3,2,1,0:T(8,128)(2,1)} %collective-permute-done.9.refs_3_), channel_id=1, source_target_pairs={{0,1},{1,0},{2,3},{3,2},{4,5},{5,4},{6,7},{7,6},{8,9},{9,8},{10,11... | collective-permute-start | bytes 1536008 | tf_op jit(solution)/shard_map/ppermute | solution.py:378
  86.5 19.9 %collective-permute-start.16 = (bf16[5,1,80,640]{3,2,1,0:T(8,128)(2,1)}, bf16[5,1,80,640]{3,2,1,0:T(8,128)(2,1)}, u32[]{:S(2)}, u32[]{:S(2)}) collective-permute-start(bf16[5,1,80,640]{3,2,1,0:T(8,128)(2,1)} %collective-permute-done.11.refs_6_), channel_id=1, source_target_pairs={{0,1},{1,0},{2,3},{3,2},{4,5},{5,4},{6,7},{7,6},{8,9},{9,8},{10,11... | collective-permute-start | bytes 1536008 | tf_op jit(solution)/shard_map/ppermute | solution.py:378
  91.2 26.8 %collective-permute-start.17 = (bf16[5,1,80,640]{3,2,1,0:T(8,128)(2,1)}, bf16[5,1,80,640]{3,2,1,0:T(8,128)(2,1)S(1)}, u32[]{:S(2)}, u32[]{:S(2)}) collective-permute-start(bf16[5,1,80,640]{3,2,1,0:T(8,128)(2,1)} %collective-permute-done.13.refs_9_), channel_id=1, source_target_pairs={{0,1},{1,0},{2,3},{3,2},{4,5},{5,4},{6,7},{7,6},{8,9},{9,8},{10,11... | collective-permute-start | bytes 1536008 | tf_op jit(solution)/shard_map/ppermute | solution.py:378
  91.7 26.3 %collective-permute-start.4 = (bf16[1,4,32,1920]{3,2,1,0:T(8,128)(2,1)}, bf16[1,4,32,1920]{3,2,1,0:T(8,128)(2,1)S(1)}, u32[]{:S(2)}, u32[]{:S(2)}) collective-permute-start(bf16[1,4,32,1920]{3,2,1,0:T(8,128)(2,1)} %shard_map.109), channel_id=1, source_target_pairs={{0,1},{1,2},{2,3},{4,5},{5,6},{6,7},{8,9},{9,10},{10,11},{12,13},{... | collective-permute-start | bytes 1474568 | tf_op jit(solution)/shard_map/ppermute | solution.py:19
  104.8 13.2 %collective-permute-start.18 = (bf16[4,1,80,640]{3,2,1,0:T(8,128)(2,1)}, bf16[4,1,80,640]{3,2,1,0:T(8,128)(2,1)S(1)}, u32[]{:S(2)}, u32[]{:S(2)}) collective-permute-start(bf16[4,1,80,640]{3,2,1,0:T(8,128)(2,1)} %collective-permute-done.10.refs_4_), channel_id=1, source_target_pairs={{0,1},{1,0},{2,3},{3,2},{4,5},{5,4},{6,7},{7,6},{8,9},{9,8},{10,11... | collective-permute-start | bytes 1228808 | tf_op jit(solution)/shard_map/ppermute | solution.py:334
  106.4 11.6 %collective-permute-start.19 = (bf16[4,1,80,640]{3,2,1,0:T(8,128)(2,1)}, bf16[4,1,80,640]{3,2,1,0:T(8,128)(2,1)S(1)}, u32[]{:S(2)}, u32[]{:S(2)}) collective-permute-start(bf16[4,1,80,640]{3,2,1,0:T(8,128)(2,1)} %collective-permute-done.12.refs_7_), channel_id=1, source_target_pairs={{0,1},{1,0},{2,3},{3,2},{4,5},{5,4},{6,7},{7,6},{8,9},{9,8},{10,11... | collective-permute-start | bytes 1228808 | tf_op jit(solution)/shard_map/ppermute | solution.py:334
  106.5 11.5 %collective-permute-start.20 = (bf16[4,1,80,640]{3,2,1,0:T(8,128)(2,1)}, bf16[4,1,80,640]{3,2,1,0:T(8,128)(2,1)S(1)}, u32[]{:S(2)}, u32[]{:S(2)}) collective-permute-start(bf16[4,1,80,640]{3,2,1,0:T(8,128)(2,1)} %collective-permute-done.14.refs_10_), channel_id=1, source_target_pairs={{0,1},{1,0},{2,3},{3,2},{4,5},{5,4},{6,7},{7,6},{8,9},{9,8},{10,11... | collective-permute-start | bytes 1228808 | tf_op jit(solution)/shard_map/ppermute | solution.py:334
  136.7 28.2 %copy-start.9 = (f32[1280]{0:T(1024)S(1)}, f32[1280]{0:T(1024)}, u32[]{:S(2)}) copy-start(f32[1280]{0:T(1024)} %param.16) | copy-start | bytes 15364
  136.7 28.8 %copy-start.10 = (f32[1280]{0:T(1024)S(1)}, f32[1280]{0:T(1024)}, u32[]{:S(2)}) copy-start(f32[1280]{0:T(1024)} %param.21) | copy-start | bytes 15364
  161.1 20.4 %all-to-all-start = ((bf16[8,4,16,640]{3,2,1,0:T(8,128)(2,1)}), bf16[8,4,16,640]{3,2,1,0:T(8,128)(2,1)S(1)}, u32[]{:S(2)}, u32[]{:S(2)}) async-start(bf16[8,4,16,640]{3,2,1,0:T(8,128)(2,1)} %get-tuple-element.15), calls=%async_computation | async-start | bytes 1310720 | tf_op jit(solution)/shard_map/all_to_all | solution.py:347
  181.5 21.1 %all-to-all-start.3 = ((bf16[8,2,16,1280]{3,2,1,0:T(8,128)(2,1)}), bf16[8,2,16,1280]{3,2,1,0:T(8,128)(2,1)S(1)}, u32[]{:S(2)}, u32[]{:S(2)}) async-start(bf16[8,2,16,1280]{3,2,1,0:T(8,128)(2,1)} %bitcast.48), calls=%async_computation.3 | async-start | bytes 1310720 | tf_op jit(solution)/shard_map/all_to_all | solution.py:351
  (11 other events, 35.3 us)

commit v2 on v1

--- a/solution.py
+++ b/solution.py
@@ -72,12 +72,12 @@
             bytes_accessed=2 * (5 * frames + 2) * rows * columns * channels,
             transcendentals=0,
         ),
-    )(*sequence, time_weight.reshape(3 * channels, channels), time_bias.reshape(1, channels))
+    )(*sequence, time_weight.reshape(3 * channels, channels), time_bias)
 
 
 def strided_kernel(spans, parts, where_ref, upper_ref, bias_ref, *refs):
     planes_refs, refs = refs[:parts], refs[parts:]
-    pieces, (*out_refs, weight, total, sems) = refs[: len(spans)], refs[len(spans) :]
+    pieces, (out_ref, weight, total, sems) = refs[: len(spans)], refs[len(spans) :]
     step = pl.program_id(0)
     _, _, frames, half_cols, width = planes_refs[0].shape
     half_rows = sum(ref.shape[0] for ref in planes_refs)
@@ -115,37 +115,35 @@
     @pl.when(step == 2)
     def _():
         done = total[...] + product(jnp.concatenate([ref[:, 0] for ref in planes_refs], axis=0), 1)
-        done = done.reshape(half_rows, frames, half_cols, done.shape[1])
-        part = half_cols // len(out_refs)
-        for chunk, out_ref in enumerate(out_refs):
-            out_ref[...] = done[:, :, chunk * part : (chunk + 1) * part].astype(jnp.bfloat16)
-
-
-def strided(planes, upper, pieces, where, bias, chunks):
-    _, frames, half_cols, width = planes[0].shape
+        out_ref[...] = done.astype(jnp.bfloat16).reshape(out_ref.shape)
+
+
+def strided(planes, upper, pieces, where, bias, chunk, chunks):
+    _, frames, all_cols, width = planes[0].shape
+    half_cols = all_cols // chunks
     outputs = bias.shape[0]
     half_rows = sum(part.shape[0] for part in planes) // 2
     count = half_rows * frames * half_cols
     unit = pieces[0].shape[2]
-    block = (half_rows, frames, half_cols // chunks, outputs)
+    block = (half_rows, frames, half_cols, outputs)
     anywhere = pl.BlockSpec(memory_space=pl.ANY)
     return pl.pallas_call(
         functools.partial(strided_kernel, tuple(piece.shape[:2] for piece in pieces), len(planes)),
-        out_shape=[jax.ShapeDtypeStruct(block, jnp.bfloat16)] * chunks,
+        out_shape=jax.ShapeDtypeStruct(block, jnp.bfloat16),
         grid=(3,),
         in_specs=[
             pl.BlockSpec(memory_space=pltpu.SMEM),
-            pl.BlockSpec((1, frames, half_cols, width), lambda a: (0, 0, 0, 0)),
+            pl.BlockSpec((1, frames, half_cols, width), lambda a: (0, 0, chunk, 0)),
             pl.BlockSpec((1, outputs), lambda a: (0, 0)),
         ]
         + [
             pl.BlockSpec(
-                (part.shape[0] // 2, 1, frames, half_cols, width), lambda a: (0, 1 - a // 2, 0, 0, 0)
+                (part.shape[0] // 2, 1, frames, half_cols, width), lambda a: (0, 1 - a // 2, 0, chunk, 0)
             )
             for part in planes
         ]
         + [anywhere] * len(pieces),
-        out_specs=[pl.BlockSpec(block, lambda a: (0, 0, 0, 0))] * chunks,
+        out_specs=pl.BlockSpec(block, lambda a: (0, 0, 0, 0)),
         scratch_shapes=[
             pltpu.VMEM((3, outputs // unit, unit, width), jnp.bfloat16),
             pltpu.VMEM((count, outputs), jnp.float32),
@@ -160,7 +158,7 @@
         where,
         upper,
         bias.reshape(1, outputs),
-        *(part.reshape(-1, 2, frames, half_cols, width) for part in planes),
+        *(part.reshape(-1, 2, frames, all_cols, width) for part in planes),
         *pieces,
     )
 
@@ -320,25 +318,24 @@
         [first[part]] + own[part] + inner[part][::-1] + [outer[part], last[part]] for part in range(len(starts))
     ]
 
-    pieces, where, distant = strided_weights(down_weight, frame, row, channels)
+    pieces, where = strided_weights(down_weight, frame, row, channels)
 
     taps = jnp.where(side == 0, time_weight, time_weight[::-1])
-    final = temporal(sequences[0], taps, time_bias, half - 1, 1, 1)
-    upper = passed_along(final, "row", 1)
-    lower_planes = temporal(sequences[0], taps, time_bias, 0, half, 2)
-    upper_planes = temporal(sequences[1], taps, time_bias, 0, half, 2)
-    lower_planes, *distant = lax.optimization_barrier([lower_planes] + distant)
+    bias_row = time_bias.reshape(1, channels)
+    lower_planes = temporal(sequences[0], taps, bias_row, 0, half, 2)
+    upper = passed_along(lower_planes[-1:], "row", 1)
+    upper_planes = temporal(sequences[1], taps, bias_row, 0, half, 2)
     planes = [upper_planes, lower_planes]
     shares = down_bias.reshape(lines, 2, down_bias.shape[0] // groups)
     bias = lax.dynamic_index_in_dim(shares, side, axis=1, keepdims=False).reshape(-1)
-    pieces += [lax.ppermute(value, "row", [(at, at ^ 1) for at in range(lax.axis_size("row"))]) for value in distant]
 
     half_rows, half_cols = rows_here // 2, columns // 2
     pixels_here = half_rows * half_cols // groups
     chunks = 2 if groups == half_rows and pixels_here % 16 == 0 else 1
     moved, results = [], []
     part = pixels_here // chunks
-    for coarse in strided(planes, upper, pieces, where, bias, chunks):
+    for at in range(chunks):
+        coarse = strided(planes, upper, pieces, where, bias, at, chunks)
         half_width = coarse.shape[-1]
         tokens = coarse
         if groups != half_rows:
@@ -363,24 +360,34 @@
     if unit % 16 or lines & (lines - 1) or row_devices % 4:
         members = [[2 * at + side for at in range(lines)] for side in range(2)]
         gathered = lax.all_gather(shard, "frame", axis=1, tiled=True, axis_index_groups=members)
-        return [gathered[:, None]], jnp.zeros((1, 2), jnp.int32), []
+        return [gathered[:, None]], jnp.zeros((1, 2), jnp.int32)
     core, plane = row % 2, row // 2 % 2
     shard = shard.reshape(9, 2, unit, channels)
-    pieces, where, distant, beyond = [shard], [(0, 2 * line)], [], []
+    pieces, where = [shard], [(0, 2 * line)]
     mine = lax.dynamic_slice(shard, (4 * plane, core, 0, 0), (5, 1, unit, channels))
     rows = range(row_devices)
+
+    def along(value, pairs):
+        steps = [(2 * source + at, 2 * target + at) for source, target in pairs for at in range(2)]
+        return lax.ppermute(value, "frame", steps)
+
+    nears = {}
     for distance in range(1, lines):
         place = 2 * (line ^ distance)
-        steps = [(at, (at // 2 ^ distance) * 2 + at % 2) for at in range(groups)]
-        near = lax.ppermute(mine, "frame", steps)
+        if lines == 4 and distance == 3:
+            middle = along(mine, [(1, 2), (2, 1)])
+            near = middle + along(nears[2], [(1, 0), (2, 3)])
+        else:
+            near = along(mine, [(at, at ^ distance) for at in range(lines)])
+        nears[distance] = near
         sent = lax.dynamic_slice_in_dim(near, plane, 4, axis=0)
         far = lax.ppermute(sent, "row", [(at, at ^ 2) for at in rows])
-        pieces += [near, far, lax.ppermute(near, "row", [(at, at ^ 1) for at in rows])]
-        where += [(4 * plane, place + core), (5 - 5 * plane, place + core), (4 * plane, place + 1 - core)]
-        distant.append(far)
-        beyond.append((5 - 5 * plane, place + 1 - core))
-    where = jnp.stack([jnp.stack([jnp.int32(tap), jnp.int32(at)]) for tap, at in where + beyond])
-    return pieces, where, distant
+        pieces += [near, far]
+        where += [(4 * plane, place + core), (5 - 5 * plane, place + core)]
+        for value, tap in ((near, 4 * plane), (far, 5 - 5 * plane)):
+            pieces.append(lax.ppermute(value, "row", [(at, at ^ 1) for at in rows]))
+            where.append((tap, place + 1 - core))
+    return pieces, jnp.stack([jnp.stack([jnp.int32(tap), jnp.int32(at)]) for tap, at in where])
 
 
 def solution(mesh):

time: 226 us -> 216 us (0.956)
  blocking collectives: 45.9 us -> 21.5 us
  waiting for transfers between devices: 36.3 us -> 51.9 us
  local copies, waits for them, and re-layouts: 17 us -> 14 us
    all_to_all x1 -> x0, blocking collectives: 24.4 us -> none  [on_device(): lax.all_to_all(tokens, 'frame', split_axis=0, concat_axis=0, tiled=True)]
    ppermute x8, waiting for transfers between devices: 2.27 us -> 20 us  [moved_along(): return lax.ppermute(value, 'frame', pairs)]
    ppermute x9 -> x10, waiting for transfers between devices: 24.2 us -> 15.4 us  [the longest x4 15.4 us: along(): return lax.ppermute(value, 'frame', steps)]
    ppermute x8, starting transfers between devices: 32.7 us -> 25.7 us  [moved_along(): return lax.ppermute(value, 'frame', pairs)]
    all_to_all x1 -> x2, waiting for transfers between devices: 3.88 us -> 10.7 us  [on_device(): lax.all_to_all(tokens, 'frame', split_axis=0, concat_axis=0, tiled=True)]
    pallas_call x1 -> x2, Pallas kernels: 17.4 us -> 23.1 us  [strided(): pl.pallas_call(functools.partial(strided_kernel, tuple((piece.shape[:2] f...]
    all_to_all x1 -> x2, starting transfers between devices: 3.76 us -> 9.27 us  [on_device(): lax.all_to_all(tokens, 'frame', split_axis=0, concat_axis=0, tiled=True)]
    dynamic_slice x3, local copies, waits for them, and re-layouts: 5.4 us -> 0.86 us  [strided_weights(): sent = lax.dynamic_slice_in_dim(near, plane, 4, axis=0)]
  transfers between devices with their start and end apart: 23 -> 25, of which waited for: 5 -> 9; matrix products, arithmetic and copies ran while one was open for 8% -> 6% of each run, Pallas kernels for 22% -> 26%
where the time goes in v2:
time: 216 us; the launch traced here: 215 us
  Pallas kernels  68.1 us (32%)
  starting transfers between devices  55.5 us (26%)
  waiting for transfers between devices  51.9 us (24%)
  blocking collectives  21.5 us (10%)
  local copies, waits for them, and re-layouts  14 us (6%)
  other arithmetic  3.73 us (2%)
    ppermute x8, starting transfers between devices, moved_along(): return lax.ppermute(value, 'frame', pairs)  25.7 us
    pallas_call x2, Pallas kernels, strided(): pl.pallas_call(functools.partial(strided_kernel, tuple((piece.shape[:2] f...  23.1 us
    pallas_call x2, Pallas kernels, attention(): pl.pallas_call(attention_kernel, out_shape=jax.ShapeDtypeStruct((frames,...  23.1 us
    pallas_call x2, Pallas kernels, temporal(): pl.pallas_call(temporal_kernel, out_shape=jax.ShapeDtypeStruct((rows, fra...  21.9 us
    all_to_all x1, blocking collectives, on_device(): lax.all_to_all(result, 'frame', split_axis=0, concat_axis=0, tiled=True)  21.5 us
    ppermute x8, waiting for transfers between devices, moved_along(): return lax.ppermute(value, 'frame', pairs)  20 us
    ppermute x4, waiting for transfers between devices, along(): return lax.ppermute(value, 'frame', steps)  15.4 us
    all_to_all x2, waiting for transfers between devices, on_device(): lax.all_to_all(tokens, 'frame', split_axis=0, concat_axis=0, tiled=True)  10.7 us
  transfers between devices with their start and end apart: 25, of which 9 were waited for; matrix products, arithmetic and copies ran while one was open for 6% of the time, Pallas kernels for 26%

profile of v2, /device:TPU:0, one launch (start us, length us, event | category | flops | bytes accessed | tf_op | source)
XLA Modules:
  0.0 215.0 jit_solution(8192987715506385738)
XLA Ops:
  0.0 1.9 constant_dynamic-slice_fusion.3
  1.9 4.1 %collective-permute-start.13 = (bf16[5,1,80,640]{3,2,1,0:T(8,128)(2,1)}, bf16[5,1,80,640]{3,2,1,0:T(8,128)(2,1)S(1)}, u32[]{:S(2)}, u32[]{:S(2)}) collective-permute-start(bf16[5,1,80,640]{3,2,1,0:T(8,128)(2,1)} %constant_dynamic-slice_fusion.3), channel_id=1, source_target_pairs={{0,16},{4,20},{8,24},{12,28},{16,0},{20,4},{24,8},{28,12},{1,17},{... | collective-permute-start | bytes 1536008 | tf_op jit(solution)/shard_map/ppermute | solution.py:372
  6.0 1.4 collective-permute-start.17
  7.4 3.4 %constant_dynamic-slice_fusion.4 = (bf16[1,8,64,640]{3,2,1,0:T(8,128)(2,1)}, bf16[1,8,64,640]{3,2,1,0:T(8,128)(2,1)}, bf16[1,8,64,640]{3,2,1,0:T(8,128)(2,1)}, bf16[1,8,64,640]{3,2,1,0:T(8,128)(2,1)}) fusion(bf16[2,16,64,640]{3,2,1,0:T(8,128)(2,1)} %param.11, s32[]{:T(128)S(6)} %select_n.64, s32[]{:T(128)S(6)} %select_n.63), kind=kLoop, calls=%fused_computation.7 | loop fusion | bytes 5242888 | tf_op jit(solution)/shard_map/dynamic_slice | solution.py:307
  10.8 1.5 collective-permute-start.5
  12.3 2.1 collective-permute-start.9
  14.9 14.8 %collective-permute-done.13.refs_7_ = bf16[5,1,80,640]{3,2,1,0:T(8,128)(2,1)S(1)} collective-permute-done((bf16[5,1,80,640]{3,2,1,0:T(8,128)(2,1)}, bf16[5,1,80,640]{3,2,1,0:T(8,128)(2,1)S(1)}, u32[]{:S(2)}, u32[]{:S(2)}) %collective-permute-start.13) | collective-permute-done | bytes 512032 | tf_op jit(solution)/shard_map/ppermute | solution.py:372
  29.7 1.8 collective-permute-start
  31.6 1.9 reverse_select_fusion
  36.8 9.6 %collective-permute-start.2 = (bf16[1,8,64,640]{3,2,1,0:T(8,128)(2,1)}, bf16[1,8,64,640]{3,2,1,0:T(8,128)(2,1)}, u32[]{:S(2)}, u32[]{:S(2)}) collective-permute-start(bf16[1,8,64,640]{3,2,1,0:T(8,128)(2,1)} %get-tuple-element.6.refs_2_), channel_id=1, source_target_pairs={{0,4},{4,0},{8,12},{12,8},{16,20},{20,16},{24,28},{28,24},{1,5},{5... | collective-permute-start | bytes 1966088 | tf_op jit(solution)/shard_map/ppermute | solution.py:310
  47.8 9.0 %collective-permute-done.refs_4_ = bf16[1,8,64,640]{3,2,1,0:T(8,128)(2,1)} collective-permute-done((bf16[1,8,64,640]{3,2,1,0:T(8,128)(2,1)}, bf16[1,8,64,640]{3,2,1,0:T(8,128)(2,1)}, u32[]{:S(2)}, u32[]{:S(2)}) %collective-permute-start) | collective-permute-done | bytes 655392 | tf_op jit(solution)/shard_map/ppermute | solution.py:310
  56.8 4.8 %collective-permute-start.1 = (bf16[1,8,64,640]{3,2,1,0:T(8,128)(2,1)}, bf16[1,8,64,640]{3,2,1,0:T(8,128)(2,1)}, u32[]{:S(2)}, u32[]{:S(2)}) collective-permute-start(bf16[1,8,64,640]{3,2,1,0:T(8,128)(2,1)} %collective-permute-done.refs_4_), channel_id=1, source_target_pairs={{0,8},{8,16},{12,4},{16,24},{20,12},{28,20},{1,9},{9,17},{13,5},{1... | collective-permute-start | bytes 1966088 | tf_op jit(solution)/shard_map/ppermute | solution.py:310
  61.8 1.6 collective-permute-start.10
  65.3 3.3 %collective-permute-done.8.refs_5_ = bf16[1,8,64,640]{3,2,1,0:T(8,128)(2,1)} collective-permute-done((bf16[1,8,64,640]{3,2,1,0:T(8,128)(2,1)}, bf16[1,8,64,640]{3,2,1,0:T(8,128)(2,1)}, u32[]{:S(2)}, u32[]{:S(2)}) %collective-permute-start.8) | collective-permute-done | bytes 655392 | tf_op jit(solution)/shard_map/ppermute | solution.py:310
  69.5 4.9 %collective-permute-start.6 = (bf16[1,8,64,640]{3,2,1,0:T(8,128)(2,1)}, bf16[1,8,64,640]{3,2,1,0:T(8,128)(2,1)}, u32[]{:S(2)}, u32[]{:S(2)}) collective-permute-start(bf16[1,8,64,640]{3,2,1,0:T(8,128)(2,1)} %collective-permute-done.5.refs_4_), channel_id=1, source_target_pairs={{0,8},{8,16},{12,4},{16,24},{20,12},{28,20},{1,9},{9,17},{13,5},{1... | collective-permute-start | bytes 1966088 | tf_op jit(solution)/shard_map/ppermute | solution.py:310
  75.1 6.9 %collective-permute-done.3.refs_5_ = bf16[1,8,64,640]{3,2,1,0:T(8,128)(2,1)} collective-permute-done((bf16[1,8,64,640]{3,2,1,0:T(8,128)(2,1)}, bf16[1,8,64,640]{3,2,1,0:T(8,128)(2,1)}, u32[]{:S(2)}, u32[]{:S(2)}) %collective-permute-start.3) | collective-permute-done | bytes 655392 | tf_op jit(solution)/shard_map/ppermute | solution.py:310
  82.0 1.5 collective-permute-start.14
  84.1 10.9 %shard_map.109 = bf16[8,4,32,1920]{3,2,1,0:T(8,128)(2,1)} custom-call(bf16[1,8,64,640]{3,2,1,0:T(8,128)(2,1)} %collective-permute-done.1.refs_0_, bf16[1,8,64,640]{3,2,1,0:T(8,128)(2,1)} %get-tuple-element.7.refs_1_, bf16[1,8,64,640]{3,2,1,0:T(8,128)(2,1)} %get-tuple-element.6.refs_2_, bf16[1,8,64,640]{3,2,1,0:T(8,128)(2,1)} %collective-permute-done.2.refs_3_, ...), custom_call_target="tpu_custom_call" | custom-call | flops 5033164800 | bytes 14417920 | tf_op jit(solution)/shard_map/pallas_call | solution.py:59
  95.0 1.9 slice.4
  97.0 2.3 %collective-permute-start.4 = (bf16[1,4,32,1920]{3,2,1,0:T(8,128)(2,1)}, bf16[1,4,32,1920]{3,2,1,0:T(8,128)(2,1)S(1)}, u32[]{:S(2)}, u32[]{:S(2)}) collective-permute-start(bf16[1,4,32,1920]{3,2,1,0:T(8,128)(2,1)} %slice.4), channel_id=1, source_target_pairs={{0,1},{1,2},{2,3},{4,5},{5,6},{6,7},{8,9},{9,10},{10,11},{12,13},{... | collective-permute-start | bytes 1474568 | tf_op jit(solution)/shard_map/ppermute | solution.py:19
  103.2 11.0 %shard_map.110 = bf16[8,4,32,1920]{3,2,1,0:T(8,128)(2,1)} custom-call(bf16[1,8,64,640]{3,2,1,0:T(8,128)(2,1)} %collective-permute-done.6.refs_0_, bf16[1,8,64,640]{3,2,1,0:T(8,128)(2,1)} %get-tuple-element.8.refs_1_, bf16[1,8,64,640]{3,2,1,0:T(8,128)(2,1)} %get-tuple-element.5.refs_2_, bf16[1,8,64,640]{3,2,1,0:T(8,128)(2,1)} %collective-permute-done.7.refs_3_, ...), custom_call_target="tpu_custom_call" | custom-call | flops 5033164800 | bytes 14417920 | tf_op jit(solution)/shard_map/pallas_call | solution.py:59
  115.3 11.6 %shard_map.111 = bf16[8,4,16,640]{3,2,1,0:T(8,128)(2,1)} custom-call(s32[13,2]{1,0:T(8,128)} %stack.159.where_ref, bf16[1,4,32,1920]{3,2,1,0:T(8,128)(2,1)} %copy-done.9, f32[1,640]{1,0:T(1,128)} %reshape_reshape.7.bias_ref, bf16[4,2,4,32,1920]{4,3,2,1,0:T(8,128)(2,1)} %bitcast.47, bf16[4,2,4,32,1920]{4,3,2,1,0:T(8,128)(2,1)} %bitcast.45, ...), custom_call_target="tpu_custom_call" | custom-call | flops 3774873600 | bytes 11960320 | tf_op jit(solution)/shard_map/pallas_call | solution.py:130
  126.8 5.6 %all-to-all-start = ((bf16[8,4,16,640]{3,2,1,0:T(8,128)(2,1)}), bf16[8,4,16,640]{3,2,1,0:T(8,128)(2,1)S(1)}, u32[]{:S(2)}, u32[]{:S(2)}) async-start(bf16[8,4,16,640]{3,2,1,0:T(8,128)(2,1)} %shard_map.111), calls=%async_computation | async-start | bytes 1310720 | tf_op jit(solution)/shard_map/all_to_all | solution.py:344
  132.5 11.6 %shard_map.113 = bf16[8,4,16,640]{3,2,1,0:T(8,128)(2,1)} custom-call(s32[13,2]{1,0:T(8,128)} %stack.159.where_ref, bf16[1,4,32,1920]{3,2,1,0:T(8,128)(2,1)} %copy-done.9, f32[1,640]{1,0:T(1,128)} %reshape_reshape.7.bias_ref, bf16[4,2,4,32,1920]{4,3,2,1,0:T(8,128)(2,1)} %bitcast.48, bf16[4,2,4,32,1920]{4,3,2,1,0:T(8,128)(2,1)} %bitcast.46, ...), custom_call_target="tpu_custom_call" | custom-call | flops 3774873600 | bytes 11960320 | tf_op jit(solution)/shard_map/pallas_call | solution.py:130
  144.1 5.9 %all-to-all-done.tokens_ref = bf16[8,4,16,640]{3,2,1,0:T(8,128)(2,1)S(1)} async-done(((bf16[8,4,16,640]{3,2,1,0:T(8,128)(2,1)}), bf16[8,4,16,640]{3,2,1,0:T(8,128)(2,1)S(1)}, u32[]{:S(2)}, u32[]{:S(2)}) %all-to-all-start) | async-done | bytes 655392 | tf_op jit(solution)/shard_map/all_to_all | solution.py:344
  150.0 3.6 %all-to-all-start.2 = ((bf16[8,4,16,640]{3,2,1,0:T(8,128)(2,1)}), bf16[8,4,16,640]{3,2,1,0:T(8,128)(2,1)S(1)}, u32[]{:S(2)}, u32[]{:S(2)}) async-start(bf16[8,4,16,640]{3,2,1,0:T(8,128)(2,1)} %shard_map.113), calls=%async_computation.2 | async-start | bytes 1310720 | tf_op jit(solution)/shard_map/all_to_all | solution.py:344
  154.9 11.5 %shard_map.112 = bf16[16,16,1280]{2,1,0:T(8,128)(2,1)} custom-call(bf16[8,4,16,640]{3,2,1,0:T(8,128)(2,1)} %copy-done.3, f32[1,1280]{1,0:T(1,128)} %reshape.38.gain_ref, f32[1,1280]{1,0:T(1,128)} %reshape.39.bias_ref, bf16[1280,1280]{1,0:T(8,128)(2,1)} %wq_hbm.3, bf16[1280,1280]{1,0:T(8,128)(2,1)} %wk_hbm.3, bf16[1280,1280]{1,0:T(8,128)(2,1)} %wv_hbm.3, ...), custom_call_target="tpu_custom_call" | custom-call | flops 3355443200 | bytes 14417920 | tf_op jit(solution)/shard_map/pallas_call | solution.py:256
  166.4 4.8 %all-to-all-done.2.tokens_ref = bf16[8,4,16,640]{3,2,1,0:T(8,128)(2,1)S(1)} async-done(((bf16[8,4,16,640]{3,2,1,0:T(8,128)(2,1)}), bf16[8,4,16,640]{3,2,1,0:T(8,128)(2,1)S(1)}, u32[]{:S(2)}, u32[]{:S(2)}) %all-to-all-start.2) | async-done | bytes 655392 | tf_op jit(solution)/shard_map/all_to_all | solution.py:344
  171.1 3.8 %all-to-all-start.1 = ((bf16[8,2,16,1280]{3,2,1,0:T(8,128)(2,1)}), bf16[8,2,16,1280]{3,2,1,0:T(8,128)(2,1)S(1)}, u32[]{:S(2)}, u32[]{:S(2)}) async-start(bf16[8,2,16,1280]{3,2,1,0:T(8,128)(2,1)} %bitcast.52), calls=%async_computation.1 | async-start | bytes 1310720 | tf_op jit(solution)/shard_map/all_to_all | solution.py:348
  174.9 11.6 %shard_map.114 = bf16[16,16,1280]{2,1,0:T(8,128)(2,1)} custom-call(bf16[8,4,16,640]{3,2,1,0:T(8,128)(2,1)} %copy-done.4, f32[1,1280]{1,0:T(1,128)} %reshape.38.gain_ref, f32[1,1280]{1,0:T(1,128)} %reshape.39.bias_ref, bf16[1280,1280]{1,0:T(8,128)(2,1)} %wq_hbm.3, bf16[1280,1280]{1,0:T(8,128)(2,1)} %wk_hbm.3, bf16[1280,1280]{1,0:T(8,128)(2,1)} %wv_hbm.3, ...), custom_call_target="tpu_custom_call" | custom-call | flops 3355443200 | bytes 14417920 | tf_op jit(solution)/shard_map/pallas_call | solution.py:256
  186.5 5.8 %all-to-all-done.1 = bf16[8,2,16,1280]{3,2,1,0:T(8,128)(2,1)S(1)} async-done(((bf16[8,2,16,1280]{3,2,1,0:T(8,128)(2,1)}), bf16[8,2,16,1280]{3,2,1,0:T(8,128)(2,1)S(1)}, u32[]{:S(2)}, u32[]{:S(2)}) %all-to-all-start.1) | async-done | bytes 655392 | tf_op jit(solution)/shard_map/all_to_all | solution.py:348
  192.2 21.5 %all_to_all.20 = bf16[8,2,16,1280]{3,2,1,0:T(8,128)(2,1)S(1)} all-to-all(bf16[8,2,16,1280]{3,2,1,0:T(8,128)(2,1)} %bitcast.53), channel_id=1, replica_groups=mesh['frame'=8,'row'=4] {'frame'}, dimensions={0} | all-to-all | bytes 1310720 | tf_op jit(solution)/shard_map/all_to_all | solution.py:348
  (79 shorter events, 17.0 us)
Async XLA Ops:
  1.9 27.8 %collective-permute-start.13 = (bf16[5,1,80,640]{3,2,1,0:T(8,128)(2,1)}, bf16[5,1,80,640]{3,2,1,0:T(8,128)(2,1)S(1)}, u32[]{:S(2)}, u32[]{:S(2)}) collective-permute-start(bf16[5,1,80,640]{3,2,1,0:T(8,128)(2,1)} %constant_dynamic-slice_fusion.3), channel_id=1, source_target_pairs={{0,16},{4,20},{8,24},{12,28},{16,0},{20,4},{24,8},{28,12},{1,17},{... | collective-permute-start | bytes 1536008 | tf_op jit(solution)/shard_map/ppermute | solution.py:372
  6.0 27.5 %collective-permute-start.17 = (bf16[5,1,80,640]{3,2,1,0:T(8,128)(2,1)}, bf16[5,1,80,640]{3,2,1,0:T(8,128)(2,1)}, u32[]{:S(2)}, u32[]{:S(2)}) collective-permute-start(bf16[5,1,80,640]{3,2,1,0:T(8,128)(2,1)} %constant_dynamic-slice_fusion.3), channel_id=1, source_target_pairs={{8,16},{12,20},{16,8},{20,12},{9,17},{13,21},{17,9},{21,13},{10,18... | collective-permute-start | bytes 1536008 | tf_op jit(solution)/shard_map/ppermute | solution.py:372
  7.4 24.1 %copy-start.5 = (bf16[3,640,640]{2,1,0:T(8,128)(2,1)S(1)}, bf16[3,640,640]{2,1,0:T(8,128)(2,1)}, u32[]{:S(2)}) copy-start(bf16[3,640,640]{2,1,0:T(8,128)(2,1)} %param.12) | copy-start | bytes 7372804
  10.8 26.0 %collective-permute-start.5 = (bf16[1,8,64,640]{3,2,1,0:T(8,128)(2,1)}, bf16[1,8,64,640]{3,2,1,0:T(8,128)(2,1)}, u32[]{:S(2)}, u32[]{:S(2)}) collective-permute-start(bf16[1,8,64,640]{3,2,1,0:T(8,128)(2,1)} %get-tuple-element.8.refs_1_), channel_id=1, source_target_pairs={{0,4},{4,0},{8,12},{12,8},{16,20},{20,16},{24,28},{28,24},{1,5},{5... | collective-permute-start | bytes 1966088 | tf_op jit(solution)/shard_map/ppermute | solution.py:310
  12.3 23.2 %collective-permute-start.9 = (bf16[5,1,80,640]{3,2,1,0:T(8,128)(2,1)}, bf16[5,1,80,640]{3,2,1,0:T(8,128)(2,1)S(1)}, u32[]{:S(2)}, u32[]{:S(2)}) collective-permute-start(bf16[5,1,80,640]{3,2,1,0:T(8,128)(2,1)} %constant_dynamic-slice_fusion.3), channel_id=1, source_target_pairs={{0,8},{4,12},{8,0},{12,4},{16,24},{20,28},{24,16},{28,20},{1,9},{5... | collective-permute-start | bytes 1536008 | tf_op jit(solution)/shard_map/ppermute | solution.py:372
  14.4 32.1 %collective-permute-start.7 = (bf16[1,8,64,640]{3,2,1,0:T(8,128)(2,1)}, bf16[1,8,64,640]{3,2,1,0:T(8,128)(2,1)}, u32[]{:S(2)}, u32[]{:S(2)}) collective-permute-start(bf16[1,8,64,640]{3,2,1,0:T(8,128)(2,1)} %get-tuple-element.5.refs_2_), channel_id=1, source_target_pairs={{0,4},{4,0},{8,12},{12,8},{16,20},{20,16},{24,28},{28,24},{1,5},{5... | collective-permute-start | bytes 1966088 | tf_op jit(solution)/shard_map/ppermute | solution.py:310
  29.7 53.7 %copy-start.1 = (bf16[5,1,80,640]{3,2,1,0:T(8,128)(2,1)}, bf16[5,1,80,640]{3,2,1,0:T(8,128)(2,1)S(1)}, u32[]{:S(2)}) copy-start(bf16[5,1,80,640]{3,2,1,0:T(8,128)(2,1)S(1)} %collective-permute-done.13.refs_7_) | copy-start | bytes 1536004
  29.7 33.7 %copy-start.14 = (f32[640]{0:T(1024)S(1)}, f32[640]{0:T(1024)}, u32[]{:S(2)}) copy-start(f32[640]{0:T(1024)} %param.13) | copy-start | bytes 7684
  29.7 27.1 %collective-permute-start = (bf16[1,8,64,640]{3,2,1,0:T(8,128)(2,1)}, bf16[1,8,64,640]{3,2,1,0:T(8,128)(2,1)}, u32[]{:S(2)}, u32[]{:S(2)}) collective-permute-start(bf16[1,8,64,640]{3,2,1,0:T(8,128)(2,1)} %get-tuple-element.7.refs_1_), channel_id=1, source_target_pairs={{0,4},{4,0},{8,12},{12,8},{16,20},{20,16},{24,28},{28,24},{1,5},{5... | collective-permute-start | bytes 1966088 | tf_op jit(solution)/shard_map/ppermute | solution.py:310
  33.5 28.3 %collective-permute-start.18 = (bf16[5,1,80,640]{3,2,1,0:T(8,128)(2,1)S(1)}, bf16[5,1,80,640]{3,2,1,0:T(8,128)(2,1)S(1)}, u32[]{:S(2)}, u32[]{:S(2)}) collective-permute-start(bf16[5,1,80,640]{3,2,1,0:T(8,128)(2,1)S(1)} %collective-permute-done.13.refs_7_), channel_id=1, source_target_pairs={{8,0},{12,4},{16,24},{20,28},{9,1},{13,5},{17,25},{21,29},{10,2},{... | collective-permute-start | bytes 1536008 | tf_op jit(solution)/shard_map/ppermute | solution.py:372
  35.5 59.5 %copy-start.2 = (bf16[5,1,80,640]{3,2,1,0:T(8,128)(2,1)}, bf16[5,1,80,640]{3,2,1,0:T(8,128)(2,1)S(1)}, u32[]{:S(2)}) copy-start(bf16[5,1,80,640]{3,2,1,0:T(8,128)(2,1)S(1)} %collective-permute-done.9.refs_3_) | copy-start | bytes 1536004
  35.5 33.1 %collective-permute-start.8 = (bf16[1,8,64,640]{3,2,1,0:T(8,128)(2,1)}, bf16[1,8,64,640]{3,2,1,0:T(8,128)(2,1)}, u32[]{:S(2)}, u32[]{:S(2)}) collective-permute-start(bf16[1,8,64,640]{3,2,1,0:T(8,128)(2,1)} %get-tuple-element.8.refs_1_), channel_id=1, source_target_pairs={{4,12},{8,0},{12,20},{16,8},{20,28},{24,16},{5,13},{9,1},{13,21},{... | collective-permute-start | bytes 1966088 | tf_op jit(solution)/shard_map/ppermute | solution.py:310
  36.8 32.6 %collective-permute-start.2 = (bf16[1,8,64,640]{3,2,1,0:T(8,128)(2,1)}, bf16[1,8,64,640]{3,2,1,0:T(8,128)(2,1)}, u32[]{:S(2)}, u32[]{:S(2)}) collective-permute-start(bf16[1,8,64,640]{3,2,1,0:T(8,128)(2,1)} %get-tuple-element.6.refs_2_), channel_id=1, source_target_pairs={{0,4},{4,0},{8,12},{12,8},{16,20},{20,16},{24,28},{28,24},{1,5},{5... | collective-permute-start | bytes 1966088 | tf_op jit(solution)/shard_map/ppermute | solution.py:310
  46.6 35.4 %collective-permute-start.3 = (bf16[1,8,64,640]{3,2,1,0:T(8,128)(2,1)}, bf16[1,8,64,640]{3,2,1,0:T(8,128)(2,1)}, u32[]{:S(2)}, u32[]{:S(2)}) collective-permute-start(bf16[1,8,64,640]{3,2,1,0:T(8,128)(2,1)} %get-tuple-element.7.refs_1_), channel_id=1, source_target_pairs={{4,12},{8,0},{12,20},{16,8},{20,28},{24,16},{5,13},{9,1},{13,21},{... | collective-permute-start | bytes 1966088 | tf_op jit(solution)/shard_map/ppermute | solution.py:310
  56.8 26.7 %collective-permute-start.1 = (bf16[1,8,64,640]{3,2,1,0:T(8,128)(2,1)}, bf16[1,8,64,640]{3,2,1,0:T(8,128)(2,1)}, u32[]{:S(2)}, u32[]{:S(2)}) collective-permute-start(bf16[1,8,64,640]{3,2,1,0:T(8,128)(2,1)} %collective-permute-done.refs_4_), channel_id=1, source_target_pairs={{0,8},{8,16},{12,4},{16,24},{20,12},{28,20},{1,9},{9,17},{13,5},{1... | collective-permute-start | bytes 1966088 | tf_op jit(solution)/shard_map/ppermute | solution.py:310
  61.8 21.7 %collective-permute-start.10 = (bf16[4,1,80,640]{3,2,1,0:T(8,128)(2,1)S(1)}, bf16[4,1,80,640]{3,2,1,0:T(8,128)(2,1)}, u32[]{:S(2)}, u32[]{:S(2)}) collective-permute-start(bf16[4,1,80,640]{3,2,1,0:T(8,128)(2,1)S(1)} %constant_dynamic-slice_fusion.2), channel_id=1, source_target_pairs={{0,2},{1,3},{2,0},{3,1},{4,6},{5,7},{6,4},{7,5},{8,10},{9,11},{10,... | collective-permute-start | bytes 1228808 | tf_op jit(solution)/shard_map/ppermute | solution.py:384
  65.3 31.6 %copy-start = (bf16[5,1,80,640]{3,2,1,0:T(8,128)(2,1)}, bf16[5,1,80,640]{3,2,1,0:T(8,128)(2,1)S(1)}, u32[]{:S(2)}) copy-start(bf16[5,1,80,640]{3,2,1,0:T(8,128)(2,1)S(1)} %add.71.refs_11_) | copy-start | bytes 1536004
  68.6 28.4 %collective-permute-start.11 = (bf16[5,1,80,640]{3,2,1,0:T(8,128)(2,1)S(1)}, bf16[5,1,80,640]{3,2,1,0:T(8,128)(2,1)S(1)}, u32[]{:S(2)}, u32[]{:S(2)}) collective-permute-start(bf16[5,1,80,640]{3,2,1,0:T(8,128)(2,1)S(1)} %collective-permute-done.9.refs_3_), channel_id=1, source_target_pairs={{0,1},{1,0},{2,3},{3,2},{4,5},{5,4},{6,7},{7,6},{8,9},{9,8},{10,11... | collective-permute-start | bytes 1536008 | tf_op jit(solution)/shard_map/ppermute | solution.py:388
  69.5 33.2 %collective-permute-start.6 = (bf16[1,8,64,640]{3,2,1,0:T(8,128)(2,1)}, bf16[1,8,64,640]{3,2,1,0:T(8,128)(2,1)}, u32[]{:S(2)}, u32[]{:S(2)}) collective-permute-start(bf16[1,8,64,640]{3,2,1,0:T(8,128)(2,1)} %collective-permute-done.5.refs_4_), channel_id=1, source_target_pairs={{0,8},{8,16},{12,4},{16,24},{20,12},{28,20},{1,9},{9,17},{13,5},{1... | collective-permute-start | bytes 1966088 | tf_op jit(solution)/shard_map/ppermute | solution.py:310
  82.0 14.9 %collective-permute-start.14 = (bf16[4,1,80,640]{3,2,1,0:T(8,128)(2,1)S(1)}, bf16[4,1,80,640]{3,2,1,0:T(8,128)(2,1)}, u32[]{:S(2)}, u32[]{:S(2)}) collective-permute-start(bf16[4,1,80,640]{3,2,1,0:T(8,128)(2,1)S(1)} %constant_dynamic-slice_fusion.1), channel_id=1, source_target_pairs={{0,2},{1,3},{2,0},{3,1},{4,6},{5,7},{6,4},{7,5},{8,10},{9,11},{10,... | collective-permute-start | bytes 1228808 | tf_op jit(solution)/shard_map/ppermute | solution.py:384
  83.5 17.9 %collective-permute-start.15 = (bf16[5,1,80,640]{3,2,1,0:T(8,128)(2,1)S(1)}, bf16[5,1,80,640]{3,2,1,0:T(8,128)(2,1)S(1)}, u32[]{:S(2)}, u32[]{:S(2)}) collective-permute-start(bf16[5,1,80,640]{3,2,1,0:T(8,128)(2,1)S(1)} %collective-permute-done.13.refs_7_), channel_id=1, source_target_pairs={{0,1},{1,0},{2,3},{3,2},{4,5},{5,4},{6,7},{7,6},{8,9},{9,8},{10,11... | collective-permute-start | bytes 1536008 | tf_op jit(solution)/shard_map/ppermute | solution.py:388
  83.5 19.2 %collective-permute-start.19 = (bf16[4,1,80,640]{3,2,1,0:T(8,128)(2,1)}, bf16[4,1,80,640]{3,2,1,0:T(8,128)(2,1)}, u32[]{:S(2)}, u32[]{:S(2)}) collective-permute-start(bf16[4,1,80,640]{3,2,1,0:T(8,128)(2,1)} %constant_dynamic-slice_fusion), channel_id=1, source_target_pairs={{0,2},{1,3},{2,0},{3,1},{4,6},{5,7},{6,4},{7,5},{8,10},{9,11},{10,... | collective-permute-start | bytes 1228808 | tf_op jit(solution)/shard_map/ppermute | solution.py:384
  96.9 17.3 %collective-permute-start.20 = (bf16[5,1,80,640]{3,2,1,0:T(8,128)(2,1)S(1)}, bf16[5,1,80,640]{3,2,1,0:T(8,128)(2,1)S(1)}, u32[]{:S(2)}, u32[]{:S(2)}) collective-permute-start(bf16[5,1,80,640]{3,2,1,0:T(8,128)(2,1)S(1)} %add.71.refs_11_), channel_id=1, source_target_pairs={{0,1},{1,0},{2,3},{3,2},{4,5},{5,4},{6,7},{7,6},{8,9},{9,8},{10,11... | collective-permute-start | bytes 1536008 | tf_op jit(solution)/shard_map/ppermute | solution.py:388
  97.0 17.2 %collective-permute-start.4 = (bf16[1,4,32,1920]{3,2,1,0:T(8,128)(2,1)}, bf16[1,4,32,1920]{3,2,1,0:T(8,128)(2,1)S(1)}, u32[]{:S(2)}, u32[]{:S(2)}) collective-permute-start(bf16[1,4,32,1920]{3,2,1,0:T(8,128)(2,1)} %slice.4), channel_id=1, source_target_pairs={{0,1},{1,2},{2,3},{4,5},{5,6},{6,7},{8,9},{9,10},{10,11},{12,13},{... | collective-permute-start | bytes 1474568 | tf_op jit(solution)/shard_map/ppermute | solution.py:19
  101.4 12.7 %collective-permute-start.12 = (bf16[4,1,80,640]{3,2,1,0:T(8,128)(2,1)}, bf16[4,1,80,640]{3,2,1,0:T(8,128)(2,1)S(1)}, u32[]{:S(2)}, u32[]{:S(2)}) collective-permute-start(bf16[4,1,80,640]{3,2,1,0:T(8,128)(2,1)} %collective-permute-done.10.refs_4_), channel_id=1, source_target_pairs={{0,1},{1,0},{2,3},{3,2},{4,5},{5,4},{6,7},{7,6},{8,9},{9,8},{10,11... | collective-permute-start | bytes 1228808 | tf_op jit(solution)/shard_map/ppermute | solution.py:388
  102.6 11.5 %collective-permute-start.16 = (bf16[4,1,80,640]{3,2,1,0:T(8,128)(2,1)}, bf16[4,1,80,640]{3,2,1,0:T(8,128)(2,1)}, u32[]{:S(2)}, u32[]{:S(2)}) collective-permute-start(bf16[4,1,80,640]{3,2,1,0:T(8,128)(2,1)} %collective-permute-done.14.refs_8_), channel_id=1, source_target_pairs={{0,1},{1,0},{2,3},{3,2},{4,5},{5,4},{6,7},{7,6},{8,9},{9,8},{10,11... | collective-permute-start | bytes 1228808 | tf_op jit(solution)/shard_map/ppermute | solution.py:388
  102.7 11.5 %collective-permute-start.21 = (bf16[4,1,80,640]{3,2,1,0:T(8,128)(2,1)}, bf16[4,1,80,640]{3,2,1,0:T(8,128)(2,1)}, u32[]{:S(2)}, u32[]{:S(2)}) collective-permute-start(bf16[4,1,80,640]{3,2,1,0:T(8,128)(2,1)} %collective-permute-done.19.refs_12_), channel_id=1, source_target_pairs={{0,1},{1,0},{2,3},{3,2},{4,5},{5,4},{6,7},{7,6},{8,9},{9,8},{10,11... | collective-permute-start | bytes 1228808 | tf_op jit(solution)/shard_map/ppermute | solution.py:388
  126.8 23.2 %all-to-all-start = ((bf16[8,4,16,640]{3,2,1,0:T(8,128)(2,1)}), bf16[8,4,16,640]{3,2,1,0:T(8,128)(2,1)S(1)}, u32[]{:S(2)}, u32[]{:S(2)}) async-start(bf16[8,4,16,640]{3,2,1,0:T(8,128)(2,1)} %shard_map.111), calls=%async_computation | async-start | bytes 1310720 | tf_op jit(solution)/shard_map/all_to_all | solution.py:344
  132.5 21.2 %copy-start.12 = (f32[1280]{0:T(1024)S(1)}, f32[1280]{0:T(1024)}, u32[]{:S(2)}) copy-start(f32[1280]{0:T(1024)} %param.16) | copy-start | bytes 15364
  132.5 21.8 %copy-start.13 = (f32[1280]{0:T(1024)S(1)}, f32[1280]{0:T(1024)}, u32[]{:S(2)}) copy-start(f32[1280]{0:T(1024)} %param.21) | copy-start | bytes 15364
  150.0 21.1 %all-to-all-start.2 = ((bf16[8,4,16,640]{3,2,1,0:T(8,128)(2,1)}), bf16[8,4,16,640]{3,2,1,0:T(8,128)(2,1)S(1)}, u32[]{:S(2)}, u32[]{:S(2)}) async-start(bf16[8,4,16,640]{3,2,1,0:T(8,128)(2,1)} %shard_map.113), calls=%async_computation.2 | async-start | bytes 1310720 | tf_op jit(solution)/shard_map/all_to_all | solution.py:344
  171.1 21.1 %all-to-all-start.1 = ((bf16[8,2,16,1280]{3,2,1,0:T(8,128)(2,1)}), bf16[8,2,16,1280]{3,2,1,0:T(8,128)(2,1)S(1)}, u32[]{:S(2)}, u32[]{:S(2)}) async-start(bf16[8,2,16,1280]{3,2,1,0:T(8,128)(2,1)} %bitcast.52), calls=%async_computation.1 | async-start | bytes 1310720 | tf_op jit(solution)/shard_map/all_to_all | solution.py:348
  (8 other events, 56.5 us)

commit v3 on v2

--- a/solution.py
+++ b/solution.py
@@ -2,6 +2,7 @@
 
 import jax
 import jax.numpy as jnp
+import numpy as np
 from jax import lax
 from jax.experimental import pallas as pl
 from jax.experimental.pallas import tpu as pltpu
@@ -363,7 +364,7 @@
         return [gathered[:, None]], jnp.zeros((1, 2), jnp.int32)
     core, plane = row % 2, row // 2 % 2
     shard = shard.reshape(9, 2, unit, channels)
-    pieces, where = [shard], [(0, 2 * line)]
+    pieces = [shard]
     mine = lax.dynamic_slice(shard, (4 * plane, core, 0, 0), (5, 1, unit, channels))
     rows = range(row_devices)
 
@@ -373,7 +374,6 @@
 
     nears = {}
     for distance in range(1, lines):
-        place = 2 * (line ^ distance)
         if lines == 4 and distance == 3:
             middle = along(mine, [(1, 2), (2, 1)])
             near = middle + along(nears[2], [(1, 0), (2, 3)])
@@ -383,11 +383,21 @@
         sent = lax.dynamic_slice_in_dim(near, plane, 4, axis=0)
         far = lax.ppermute(sent, "row", [(at, at ^ 2) for at in rows])
         pieces += [near, far]
-        where += [(4 * plane, place + core), (5 - 5 * plane, place + core)]
-        for value, tap in ((near, 4 * plane), (far, 5 - 5 * plane)):
+        for value in (near, far):
             pieces.append(lax.ppermute(value, "row", [(at, at ^ 1) for at in rows]))
-            where.append((tap, place + 1 - core))
-    return pieces, jnp.stack([jnp.stack([jnp.int32(tap), jnp.int32(at)]) for tap, at in where])
+
+    def places(line, plane, core):
+        found = [(0, 2 * line)]
+        for distance in range(1, lines):
+            for half in (core, 1 - core):
+                at = 2 * (line ^ distance) + half
+                found += [(4 * plane, at), (5 - 5 * plane, at)]
+        return found
+
+    table = [places(at // 4, at // 2 % 2, at % 2) for at in range(4 * lines)]
+    table = jnp.asarray(np.array(table, np.int32))
+    where = lax.dynamic_index_in_dim(table, 4 * line + 2 * plane + core, 0, keepdims=False)
+    return pieces, where
 
 
 def solution(mesh):

time: 216 us -> 216 us (level)
  starting transfers between devices: 55.5 us -> 48.1 us
  waiting for transfers between devices: 51.9 us -> 58.9 us
    ppermute x4, waiting for transfers between devices: 15.4 us -> 26.1 us  [along(): return lax.ppermute(value, 'frame', steps)]
    ppermute x8, starting transfers between devices: 25.7 us -> 20.4 us  [moved_along(): return lax.ppermute(value, 'frame', pairs)]
    ppermute x8, waiting for transfers between devices: 20 us -> 16.3 us  [moved_along(): return lax.ppermute(value, 'frame', pairs)]
where the time goes in v3:
time: 216 us; the launch traced here: 215 us
  Pallas kernels  68.1 us (32%)
  waiting for transfers between devices  58.9 us (27%)
  starting transfers between devices  48.1 us (22%)
  blocking collectives  21.5 us (10%)
  local copies, waits for them, and re-layouts  14.9 us (7%)
  other arithmetic  3.32 us (2%)
    ppermute x4, waiting for transfers between devices, along(): return lax.ppermute(value, 'frame', steps)  26.1 us
    pallas_call x2, Pallas kernels, strided(): pl.pallas_call(functools.partial(strided_kernel, tuple((piece.shape[:2] f...  23.1 us
    pallas_call x2, Pallas kernels, attention(): pl.pallas_call(attention_kernel, out_shape=jax.ShapeDtypeStruct((frames,...  23.1 us
    pallas_call x2, Pallas kernels, temporal(): pl.pallas_call(temporal_kernel, out_shape=jax.ShapeDtypeStruct((rows, fra...  21.9 us
    all_to_all x1, blocking collectives, on_device(): lax.all_to_all(result, 'frame', split_axis=0, concat_axis=0, tiled=True)  21.5 us
    ppermute x8, starting transfers between devices, moved_along(): return lax.ppermute(value, 'frame', pairs)  20.4 us
    ppermute x8, waiting for transfers between devices, moved_along(): return lax.ppermute(value, 'frame', pairs)  16.3 us
    all_to_all x2, waiting for transfers between devices, on_device(): lax.all_to_all(tokens, 'frame', split_axis=0, concat_axis=0, tiled=True)  10.7 us
  transfers between devices with their start and end apart: 25, of which 9 were waited for; matrix products, arithmetic and copies ran while one was open for 6% of the time, Pallas kernels for 26%

profile of v3, /device:TPU:0, one launch (start us, length us, event | category | flops | bytes accessed | tf_op | source)
XLA Modules:
  0.0 215.1 jit_solution(18021419566520286803)
XLA Ops:
  0.0 1.9 constant_dynamic-slice_fusion.3
  1.9 4.1 %collective-permute-start.13 = (bf16[5,1,80,640]{3,2,1,0:T(8,128)(2,1)}, bf16[5,1,80,640]{3,2,1,0:T(8,128)(2,1)S(1)}, u32[]{:S(2)}, u32[]{:S(2)}) collective-permute-start(bf16[5,1,80,640]{3,2,1,0:T(8,128)(2,1)} %constant_dynamic-slice_fusion.3), channel_id=1, source_target_pairs={{0,16},{4,20},{8,24},{12,28},{16,0},{20,4},{24,8},{28,12},{1,17},{... | collective-permute-start | bytes 1536008 | tf_op jit(solution)/shard_map/ppermute | solution.py:373
  6.0 1.4 collective-permute-start.17
  7.4 3.4 %constant_dynamic-slice_fusion.4 = (bf16[1,8,64,640]{3,2,1,0:T(8,128)(2,1)}, bf16[1,8,64,640]{3,2,1,0:T(8,128)(2,1)}, bf16[1,8,64,640]{3,2,1,0:T(8,128)(2,1)}, bf16[1,8,64,640]{3,2,1,0:T(8,128)(2,1)}) fusion(bf16[2,16,64,640]{3,2,1,0:T(8,128)(2,1)} %param.12, s32[]{:T(128)S(6)} %select_n.69, s32[]{:T(128)S(6)} %select_n.68), kind=kLoop, calls=%fused_computation.7 | loop fusion | bytes 5242888 | tf_op jit(solution)/shard_map/dynamic_slice | solution.py:308
  10.8 1.5 collective-permute-start.5
  12.9 1.5 collective-permute-start
  14.4 15.3 %collective-permute-done.13.refs_7_ = bf16[5,1,80,640]{3,2,1,0:T(8,128)(2,1)S(1)} collective-permute-done((bf16[5,1,80,640]{3,2,1,0:T(8,128)(2,1)}, bf16[5,1,80,640]{3,2,1,0:T(8,128)(2,1)S(1)}, u32[]{:S(2)}, u32[]{:S(2)}) %collective-permute-start.13) | collective-permute-done | bytes 512032 | tf_op jit(solution)/shard_map/ppermute | solution.py:373
  31.0 10.8 %collective-permute-done.9.refs_3_ = bf16[5,1,80,640]{3,2,1,0:T(8,128)(2,1)S(1)} collective-permute-done((bf16[5,1,80,640]{3,2,1,0:T(8,128)(2,1)}, bf16[5,1,80,640]{3,2,1,0:T(8,128)(2,1)S(1)}, u32[]{:S(2)}, u32[]{:S(2)}) %collective-permute-start.9) | collective-permute-done | bytes 512032 | tf_op jit(solution)/shard_map/ppermute | solution.py:373
  43.2 4.6 %collective-permute-start.2 = (bf16[1,8,64,640]{3,2,1,0:T(8,128)(2,1)}, bf16[1,8,64,640]{3,2,1,0:T(8,128)(2,1)}, u32[]{:S(2)}, u32[]{:S(2)}) collective-permute-start(bf16[1,8,64,640]{3,2,1,0:T(8,128)(2,1)} %get-tuple-element.6.refs_2_), channel_id=1, source_target_pairs={{0,4},{4,0},{8,12},{12,8},{16,20},{20,16},{24,28},{28,24},{1,5},{5... | collective-permute-start | bytes 1966088 | tf_op jit(solution)/shard_map/ppermute | solution.py:311
  49.1 7.8 %collective-permute-done.refs_4_ = bf16[1,8,64,640]{3,2,1,0:T(8,128)(2,1)} collective-permute-done((bf16[1,8,64,640]{3,2,1,0:T(8,128)(2,1)}, bf16[1,8,64,640]{3,2,1,0:T(8,128)(2,1)}, u32[]{:S(2)}, u32[]{:S(2)}) %collective-permute-start) | collective-permute-done | bytes 655392 | tf_op jit(solution)/shard_map/ppermute | solution.py:311
  56.8 4.8 %collective-permute-start.1 = (bf16[1,8,64,640]{3,2,1,0:T(8,128)(2,1)}, bf16[1,8,64,640]{3,2,1,0:T(8,128)(2,1)}, u32[]{:S(2)}, u32[]{:S(2)}) collective-permute-start(bf16[1,8,64,640]{3,2,1,0:T(8,128)(2,1)} %collective-permute-done.refs_4_), channel_id=1, source_target_pairs={{0,8},{8,16},{12,4},{16,24},{20,12},{28,20},{1,9},{9,17},{13,5},{1... | collective-permute-start | bytes 1966088 | tf_op jit(solution)/shard_map/ppermute | solution.py:311
  62.5 1.5 collective-permute-start.10
  64.0 1.9 reverse_select_fusion
  66.5 1.3 add.54.refs_11_
  69.5 4.8 %collective-permute-start.6 = (bf16[1,8,64,640]{3,2,1,0:T(8,128)(2,1)}, bf16[1,8,64,640]{3,2,1,0:T(8,128)(2,1)}, u32[]{:S(2)}, u32[]{:S(2)}) collective-permute-start(bf16[1,8,64,640]{3,2,1,0:T(8,128)(2,1)} %collective-permute-done.5.refs_4_), channel_id=1, source_target_pairs={{0,8},{8,16},{12,4},{16,24},{20,12},{28,20},{1,9},{9,17},{13,5},{1... | collective-permute-start | bytes 1966088 | tf_op jit(solution)/shard_map/ppermute | solution.py:311
  75.1 6.8 %collective-permute-done.3.refs_5_ = bf16[1,8,64,640]{3,2,1,0:T(8,128)(2,1)} collective-permute-done((bf16[1,8,64,640]{3,2,1,0:T(8,128)(2,1)}, bf16[1,8,64,640]{3,2,1,0:T(8,128)(2,1)}, u32[]{:S(2)}, u32[]{:S(2)}) %collective-permute-start.3) | collective-permute-done | bytes 655392 | tf_op jit(solution)/shard_map/ppermute | solution.py:311
  81.9 1.5 collective-permute-start.14
  84.0 10.9 %shard_map.118 = bf16[8,4,32,1920]{3,2,1,0:T(8,128)(2,1)} custom-call(bf16[1,8,64,640]{3,2,1,0:T(8,128)(2,1)} %collective-permute-done.1.refs_0_, bf16[1,8,64,640]{3,2,1,0:T(8,128)(2,1)} %get-tuple-element.7.refs_1_, bf16[1,8,64,640]{3,2,1,0:T(8,128)(2,1)} %get-tuple-element.6.refs_2_, bf16[1,8,64,640]{3,2,1,0:T(8,128)(2,1)} %collective-permute-done.2.refs_3_, ...), custom_call_target="tpu_custom_call" | custom-call | flops 5033164800 | bytes 14417920 | tf_op jit(solution)/shard_map/pallas_call | solution.py:60
  95.0 1.8 slice.4
  97.0 2.3 %collective-permute-start.4 = (bf16[1,4,32,1920]{3,2,1,0:T(8,128)(2,1)}, bf16[1,4,32,1920]{3,2,1,0:T(8,128)(2,1)S(1)}, u32[]{:S(2)}, u32[]{:S(2)}) collective-permute-start(bf16[1,4,32,1920]{3,2,1,0:T(8,128)(2,1)} %slice.4), channel_id=1, source_target_pairs={{0,1},{1,2},{2,3},{4,5},{5,6},{6,7},{8,9},{9,10},{10,11},{12,13},{... | collective-permute-start | bytes 1474568 | tf_op jit(solution)/shard_map/ppermute | solution.py:20
  103.2 11.0 %shard_map.119 = bf16[8,4,32,1920]{3,2,1,0:T(8,128)(2,1)} custom-call(bf16[1,8,64,640]{3,2,1,0:T(8,128)(2,1)} %collective-permute-done.6.refs_0_, bf16[1,8,64,640]{3,2,1,0:T(8,128)(2,1)} %get-tuple-element.8.refs_1_, bf16[1,8,64,640]{3,2,1,0:T(8,128)(2,1)} %get-tuple-element.5.refs_2_, bf16[1,8,64,640]{3,2,1,0:T(8,128)(2,1)} %collective-permute-done.7.refs_3_, ...), custom_call_target="tpu_custom_call" | custom-call | flops 5033164800 | bytes 14417920 | tf_op jit(solution)/shard_map/pallas_call | solution.py:60
  115.3 11.6 %shard_map.120 = bf16[8,4,16,640]{3,2,1,0:T(8,128)(2,1)} custom-call(s32[13,2]{1,0:T(8,128)} %copy.21.where_ref, bf16[1,4,32,1920]{3,2,1,0:T(8,128)(2,1)} %copy-done.9, f32[1,640]{1,0:T(1,128)} %reshape_reshape.7.bias_ref, bf16[4,2,4,32,1920]{4,3,2,1,0:T(8,128)(2,1)} %bitcast.14, bf16[4,2,4,32,1920]{4,3,2,1,0:T(8,128)(2,1)} %bitcast.12, ...), custom_call_target="tpu_custom_call" | custom-call | flops 3774873600 | bytes 11960320 | tf_op jit(solution)/shard_map/pallas_call | solution.py:131
  126.9 5.7 %all-to-all-start = ((bf16[8,4,16,640]{3,2,1,0:T(8,128)(2,1)}), bf16[8,4,16,640]{3,2,1,0:T(8,128)(2,1)S(1)}, u32[]{:S(2)}, u32[]{:S(2)}) async-start(bf16[8,4,16,640]{3,2,1,0:T(8,128)(2,1)} %shard_map.120), calls=%async_computation | async-start | bytes 1310720 | tf_op jit(solution)/shard_map/all_to_all | solution.py:345
  132.6 11.6 %shard_map.122 = bf16[8,4,16,640]{3,2,1,0:T(8,128)(2,1)} custom-call(s32[13,2]{1,0:T(8,128)} %copy.21.where_ref, bf16[1,4,32,1920]{3,2,1,0:T(8,128)(2,1)} %copy-done.9, f32[1,640]{1,0:T(1,128)} %reshape_reshape.7.bias_ref, bf16[4,2,4,32,1920]{4,3,2,1,0:T(8,128)(2,1)} %bitcast.15, bf16[4,2,4,32,1920]{4,3,2,1,0:T(8,128)(2,1)} %bitcast.13, ...), custom_call_target="tpu_custom_call" | custom-call | flops 3774873600 | bytes 11960320 | tf_op jit(solution)/shard_map/pallas_call | solution.py:131
  144.2 5.9 %all-to-all-done.tokens_ref = bf16[8,4,16,640]{3,2,1,0:T(8,128)(2,1)S(1)} async-done(((bf16[8,4,16,640]{3,2,1,0:T(8,128)(2,1)}), bf16[8,4,16,640]{3,2,1,0:T(8,128)(2,1)S(1)}, u32[]{:S(2)}, u32[]{:S(2)}) %all-to-all-start) | async-done | bytes 655392 | tf_op jit(solution)/shard_map/all_to_all | solution.py:345
  150.1 3.6 %all-to-all-start.2 = ((bf16[8,4,16,640]{3,2,1,0:T(8,128)(2,1)}), bf16[8,4,16,640]{3,2,1,0:T(8,128)(2,1)S(1)}, u32[]{:S(2)}, u32[]{:S(2)}) async-start(bf16[8,4,16,640]{3,2,1,0:T(8,128)(2,1)} %shard_map.122), calls=%async_computation.2 | async-start | bytes 1310720 | tf_op jit(solution)/shard_map/all_to_all | solution.py:345
  154.9 11.5 %shard_map.121 = bf16[16,16,1280]{2,1,0:T(8,128)(2,1)} custom-call(bf16[8,4,16,640]{3,2,1,0:T(8,128)(2,1)} %copy-done.3, f32[1,1280]{1,0:T(1,128)} %reshape.38.gain_ref, f32[1,1280]{1,0:T(1,128)} %reshape.39.bias_ref, bf16[1280,1280]{1,0:T(8,128)(2,1)} %wq_hbm.3, bf16[1280,1280]{1,0:T(8,128)(2,1)} %wk_hbm.3, bf16[1280,1280]{1,0:T(8,128)(2,1)} %wv_hbm.3, ...), custom_call_target="tpu_custom_call" | custom-call | flops 3355443200 | bytes 14417920 | tf_op jit(solution)/shard_map/pallas_call | solution.py:257
  166.5 4.8 %all-to-all-done.2.tokens_ref = bf16[8,4,16,640]{3,2,1,0:T(8,128)(2,1)S(1)} async-done(((bf16[8,4,16,640]{3,2,1,0:T(8,128)(2,1)}), bf16[8,4,16,640]{3,2,1,0:T(8,128)(2,1)S(1)}, u32[]{:S(2)}, u32[]{:S(2)}) %all-to-all-start.2) | async-done | bytes 655392 | tf_op jit(solution)/shard_map/all_to_all | solution.py:345
  171.2 3.8 %all-to-all-start.1 = ((bf16[8,2,16,1280]{3,2,1,0:T(8,128)(2,1)}), bf16[8,2,16,1280]{3,2,1,0:T(8,128)(2,1)S(1)}, u32[]{:S(2)}, u32[]{:S(2)}) async-start(bf16[8,2,16,1280]{3,2,1,0:T(8,128)(2,1)} %bitcast.19), calls=%async_computation.1 | async-start | bytes 1310720 | tf_op jit(solution)/shard_map/all_to_all | solution.py:349
  175.0 11.6 %shard_map.123 = bf16[16,16,1280]{2,1,0:T(8,128)(2,1)} custom-call(bf16[8,4,16,640]{3,2,1,0:T(8,128)(2,1)} %copy-done.4, f32[1,1280]{1,0:T(1,128)} %reshape.38.gain_ref, f32[1,1280]{1,0:T(1,128)} %reshape.39.bias_ref, bf16[1280,1280]{1,0:T(8,128)(2,1)} %wq_hbm.3, bf16[1280,1280]{1,0:T(8,128)(2,1)} %wk_hbm.3, bf16[1280,1280]{1,0:T(8,128)(2,1)} %wv_hbm.3, ...), custom_call_target="tpu_custom_call" | custom-call | flops 3355443200 | bytes 14417920 | tf_op jit(solution)/shard_map/pallas_call | solution.py:257
  186.6 5.8 %all-to-all-done.1 = bf16[8,2,16,1280]{3,2,1,0:T(8,128)(2,1)S(1)} async-done(((bf16[8,2,16,1280]{3,2,1,0:T(8,128)(2,1)}), bf16[8,2,16,1280]{3,2,1,0:T(8,128)(2,1)S(1)}, u32[]{:S(2)}, u32[]{:S(2)}) %all-to-all-start.1) | async-done | bytes 655392 | tf_op jit(solution)/shard_map/all_to_all | solution.py:349
  192.3 21.5 %all_to_all.20 = bf16[8,2,16,1280]{3,2,1,0:T(8,128)(2,1)S(1)} all-to-all(bf16[8,2,16,1280]{3,2,1,0:T(8,128)(2,1)} %bitcast.20), channel_id=1, replica_groups=mesh['frame'=8,'row'=4] {'frame'}, dimensions={0} | all-to-all | bytes 1310720 | tf_op jit(solution)/shard_map/all_to_all | solution.py:349
  (75 shorter events, 16.5 us)
Async XLA Ops:
  1.9 27.8 %collective-permute-start.13 = (bf16[5,1,80,640]{3,2,1,0:T(8,128)(2,1)}, bf16[5,1,80,640]{3,2,1,0:T(8,128)(2,1)S(1)}, u32[]{:S(2)}, u32[]{:S(2)}) collective-permute-start(bf16[5,1,80,640]{3,2,1,0:T(8,128)(2,1)} %constant_dynamic-slice_fusion.3), channel_id=1, source_target_pairs={{0,16},{4,20},{8,24},{12,28},{16,0},{20,4},{24,8},{28,12},{1,17},{... | collective-permute-start | bytes 1536008 | tf_op jit(solution)/shard_map/ppermute | solution.py:373
  6.0 23.8 %collective-permute-start.17 = (bf16[5,1,80,640]{3,2,1,0:T(8,128)(2,1)}, bf16[5,1,80,640]{3,2,1,0:T(8,128)(2,1)}, u32[]{:S(2)}, u32[]{:S(2)}) collective-permute-start(bf16[5,1,80,640]{3,2,1,0:T(8,128)(2,1)} %constant_dynamic-slice_fusion.3), channel_id=1, source_target_pairs={{8,16},{12,20},{16,8},{20,12},{9,17},{13,21},{17,9},{21,13},{10,18... | collective-permute-start | bytes 1536008 | tf_op jit(solution)/shard_map/ppermute | solution.py:373
  7.4 56.6 %copy-start.5 = (bf16[3,640,640]{2,1,0:T(8,128)(2,1)S(1)}, bf16[3,640,640]{2,1,0:T(8,128)(2,1)}, u32[]{:S(2)}) copy-start(bf16[3,640,640]{2,1,0:T(8,128)(2,1)} %param.13) | copy-start | bytes 7372804
  10.8 32.3 %collective-permute-start.5 = (bf16[1,8,64,640]{3,2,1,0:T(8,128)(2,1)}, bf16[1,8,64,640]{3,2,1,0:T(8,128)(2,1)}, u32[]{:S(2)}, u32[]{:S(2)}) collective-permute-start(bf16[1,8,64,640]{3,2,1,0:T(8,128)(2,1)} %get-tuple-element.8.refs_1_), channel_id=1, source_target_pairs={{0,4},{4,0},{8,12},{12,8},{16,20},{20,16},{24,28},{28,24},{1,5},{5... | collective-permute-start | bytes 1966088 | tf_op jit(solution)/shard_map/ppermute | solution.py:311
  12.3 35.4 %collective-permute-start.7 = (bf16[1,8,64,640]{3,2,1,0:T(8,128)(2,1)}, bf16[1,8,64,640]{3,2,1,0:T(8,128)(2,1)}, u32[]{:S(2)}, u32[]{:S(2)}) collective-permute-start(bf16[1,8,64,640]{3,2,1,0:T(8,128)(2,1)} %get-tuple-element.5.refs_2_), channel_id=1, source_target_pairs={{0,4},{4,0},{8,12},{12,8},{16,20},{20,16},{24,28},{28,24},{1,5},{5... | collective-permute-start | bytes 1966088 | tf_op jit(solution)/shard_map/ppermute | solution.py:311
  12.9 44.0 %collective-permute-start = (bf16[1,8,64,640]{3,2,1,0:T(8,128)(2,1)}, bf16[1,8,64,640]{3,2,1,0:T(8,128)(2,1)}, u32[]{:S(2)}, u32[]{:S(2)}) collective-permute-start(bf16[1,8,64,640]{3,2,1,0:T(8,128)(2,1)} %get-tuple-element.7.refs_1_), channel_id=1, source_target_pairs={{0,4},{4,0},{8,12},{12,8},{16,20},{20,16},{24,28},{28,24},{1,5},{5... | collective-permute-start | bytes 1966088 | tf_op jit(solution)/shard_map/ppermute | solution.py:311
  29.7 53.7 %copy-start.1 = (bf16[5,1,80,640]{3,2,1,0:T(8,128)(2,1)}, bf16[5,1,80,640]{3,2,1,0:T(8,128)(2,1)S(1)}, u32[]{:S(2)}) copy-start(bf16[5,1,80,640]{3,2,1,0:T(8,128)(2,1)S(1)} %collective-permute-done.13.refs_7_) | copy-start | bytes 1536004
  29.7 12.2 %collective-permute-start.9 = (bf16[5,1,80,640]{3,2,1,0:T(8,128)(2,1)}, bf16[5,1,80,640]{3,2,1,0:T(8,128)(2,1)S(1)}, u32[]{:S(2)}, u32[]{:S(2)}) collective-permute-start(bf16[5,1,80,640]{3,2,1,0:T(8,128)(2,1)} %constant_dynamic-slice_fusion.3), channel_id=1, source_target_pairs={{0,8},{4,12},{8,0},{12,4},{16,24},{20,28},{24,16},{28,20},{1,9},{5... | collective-permute-start | bytes 1536008 | tf_op jit(solution)/shard_map/ppermute | solution.py:373
  29.8 32.7 %collective-permute-start.18 = (bf16[5,1,80,640]{3,2,1,0:T(8,128)(2,1)S(1)}, bf16[5,1,80,640]{3,2,1,0:T(8,128)(2,1)}, u32[]{:S(2)}, u32[]{:S(2)}) collective-permute-start(bf16[5,1,80,640]{3,2,1,0:T(8,128)(2,1)S(1)} %collective-permute-done.13.refs_7_), channel_id=1, source_target_pairs={{8,0},{12,4},{16,24},{20,28},{9,1},{13,5},{17,25},{21,29},{10,2},{... | collective-permute-start | bytes 1536008 | tf_op jit(solution)/shard_map/ppermute | solution.py:373
  41.9 26.7 %copy-start.2 = (bf16[5,1,80,640]{3,2,1,0:T(8,128)(2,1)}, bf16[5,1,80,640]{3,2,1,0:T(8,128)(2,1)S(1)}, u32[]{:S(2)}) copy-start(bf16[5,1,80,640]{3,2,1,0:T(8,128)(2,1)S(1)} %collective-permute-done.9.refs_3_) | copy-start | bytes 1536004
  41.9 26.7 %collective-permute-start.8 = (bf16[1,8,64,640]{3,2,1,0:T(8,128)(2,1)}, bf16[1,8,64,640]{3,2,1,0:T(8,128)(2,1)}, u32[]{:S(2)}, u32[]{:S(2)}) collective-permute-start(bf16[1,8,64,640]{3,2,1,0:T(8,128)(2,1)} %get-tuple-element.8.refs_1_), channel_id=1, source_target_pairs={{4,12},{8,0},{12,20},{16,8},{20,28},{24,16},{5,13},{9,1},{13,21},{... | collective-permute-start | bytes 1966088 | tf_op jit(solution)/shard_map/ppermute | solution.py:311
  43.2 26.3 %collective-permute-start.2 = (bf16[1,8,64,640]{3,2,1,0:T(8,128)(2,1)}, bf16[1,8,64,640]{3,2,1,0:T(8,128)(2,1)}, u32[]{:S(2)}, u32[]{:S(2)}) collective-permute-start(bf16[1,8,64,640]{3,2,1,0:T(8,128)(2,1)} %get-tuple-element.6.refs_2_), channel_id=1, source_target_pairs={{0,4},{4,0},{8,12},{12,8},{16,20},{20,16},{24,28},{28,24},{1,5},{5... | collective-permute-start | bytes 1966088 | tf_op jit(solution)/shard_map/ppermute | solution.py:311
  47.8 34.1 %collective-permute-start.3 = (bf16[1,8,64,640]{3,2,1,0:T(8,128)(2,1)}, bf16[1,8,64,640]{3,2,1,0:T(8,128)(2,1)}, u32[]{:S(2)}, u32[]{:S(2)}) collective-permute-start(bf16[1,8,64,640]{3,2,1,0:T(8,128)(2,1)} %get-tuple-element.7.refs_1_), channel_id=1, source_target_pairs={{4,12},{8,0},{12,20},{16,8},{20,28},{24,16},{5,13},{9,1},{13,21},{... | collective-permute-start | bytes 1966088 | tf_op jit(solution)/shard_map/ppermute | solution.py:311
  56.8 26.6 %collective-permute-start.1 = (bf16[1,8,64,640]{3,2,1,0:T(8,128)(2,1)}, bf16[1,8,64,640]{3,2,1,0:T(8,128)(2,1)}, u32[]{:S(2)}, u32[]{:S(2)}) collective-permute-start(bf16[1,8,64,640]{3,2,1,0:T(8,128)(2,1)} %collective-permute-done.refs_4_), channel_id=1, source_target_pairs={{0,8},{8,16},{12,4},{16,24},{20,12},{28,20},{1,9},{9,17},{13,5},{1... | collective-permute-start | bytes 1966088 | tf_op jit(solution)/shard_map/ppermute | solution.py:311
  62.5 20.9 %collective-permute-start.10 = (bf16[4,1,80,640]{3,2,1,0:T(8,128)(2,1)}, bf16[4,1,80,640]{3,2,1,0:T(8,128)(2,1)}, u32[]{:S(2)}, u32[]{:S(2)}) collective-permute-start(bf16[4,1,80,640]{3,2,1,0:T(8,128)(2,1)} %constant_dynamic-slice_fusion.2), channel_id=1, source_target_pairs={{0,2},{1,3},{2,0},{3,1},{4,6},{5,7},{6,4},{7,5},{8,10},{9,11},{10,... | collective-permute-start | bytes 1228808 | tf_op jit(solution)/shard_map/ppermute | solution.py:384
  67.8 29.0 %copy-start = (bf16[5,1,80,640]{3,2,1,0:T(8,128)(2,1)}, bf16[5,1,80,640]{3,2,1,0:T(8,128)(2,1)S(1)}, u32[]{:S(2)}) copy-start(bf16[5,1,80,640]{3,2,1,0:T(8,128)(2,1)S(1)} %add.54.refs_11_) | copy-start | bytes 1536004
  68.6 28.5 %collective-permute-start.11 = (bf16[5,1,80,640]{3,2,1,0:T(8,128)(2,1)S(1)}, bf16[5,1,80,640]{3,2,1,0:T(8,128)(2,1)S(1)}, u32[]{:S(2)}, u32[]{:S(2)}) collective-permute-start(bf16[5,1,80,640]{3,2,1,0:T(8,128)(2,1)S(1)} %collective-permute-done.9.refs_3_), channel_id=1, source_target_pairs={{0,1},{1,0},{2,3},{3,2},{4,5},{5,4},{6,7},{7,6},{8,9},{9,8},{10,11... | collective-permute-start | bytes 1536008 | tf_op jit(solution)/shard_map/ppermute | solution.py:387
  69.5 33.3 %collective-permute-start.6 = (bf16[1,8,64,640]{3,2,1,0:T(8,128)(2,1)}, bf16[1,8,64,640]{3,2,1,0:T(8,128)(2,1)}, u32[]{:S(2)}, u32[]{:S(2)}) collective-permute-start(bf16[1,8,64,640]{3,2,1,0:T(8,128)(2,1)} %collective-permute-done.5.refs_4_), channel_id=1, source_target_pairs={{0,8},{8,16},{12,4},{16,24},{20,12},{28,20},{1,9},{9,17},{13,5},{1... | collective-permute-start | bytes 1966088 | tf_op jit(solution)/shard_map/ppermute | solution.py:311
  81.9 14.9 %collective-permute-start.14 = (bf16[4,1,80,640]{3,2,1,0:T(8,128)(2,1)S(1)}, bf16[4,1,80,640]{3,2,1,0:T(8,128)(2,1)S(1)}, u32[]{:S(2)}, u32[]{:S(2)}) collective-permute-start(bf16[4,1,80,640]{3,2,1,0:T(8,128)(2,1)S(1)} %constant_dynamic-slice_fusion.1), channel_id=1, source_target_pairs={{0,2},{1,3},{2,0},{3,1},{4,6},{5,7},{6,4},{7,5},{8,10},{9,11},{10,... | collective-permute-start | bytes 1228808 | tf_op jit(solution)/shard_map/ppermute | solution.py:384
  83.4 18.1 %collective-permute-start.15 = (bf16[5,1,80,640]{3,2,1,0:T(8,128)(2,1)S(1)}, bf16[5,1,80,640]{3,2,1,0:T(8,128)(2,1)S(1)}, u32[]{:S(2)}, u32[]{:S(2)}) collective-permute-start(bf16[5,1,80,640]{3,2,1,0:T(8,128)(2,1)S(1)} %collective-permute-done.13.refs_7_), channel_id=1, source_target_pairs={{0,1},{1,0},{2,3},{3,2},{4,5},{5,4},{6,7},{7,6},{8,9},{9,8},{10,11... | collective-permute-start | bytes 1536008 | tf_op jit(solution)/shard_map/ppermute | solution.py:387
  83.4 19.4 %collective-permute-start.19 = (bf16[4,1,80,640]{3,2,1,0:T(8,128)(2,1)}, bf16[4,1,80,640]{3,2,1,0:T(8,128)(2,1)}, u32[]{:S(2)}, u32[]{:S(2)}) collective-permute-start(bf16[4,1,80,640]{3,2,1,0:T(8,128)(2,1)} %constant_dynamic-slice_fusion), channel_id=1, source_target_pairs={{0,2},{1,3},{2,0},{3,1},{4,6},{5,7},{6,4},{7,5},{8,10},{9,11},{10,... | collective-permute-start | bytes 1228808 | tf_op jit(solution)/shard_map/ppermute | solution.py:384
  96.8 17.4 %copy-start.10 = (bf16[4,1,80,640]{3,2,1,0:T(8,128)(2,1)}, bf16[4,1,80,640]{3,2,1,0:T(8,128)(2,1)S(1)}, u32[]{:S(2)}) copy-start(bf16[4,1,80,640]{3,2,1,0:T(8,128)(2,1)S(1)} %collective-permute-done.14.refs_8_) | copy-start | bytes 1228804
  96.8 17.5 %collective-permute-start.20 = (bf16[5,1,80,640]{3,2,1,0:T(8,128)(2,1)S(1)}, bf16[5,1,80,640]{3,2,1,0:T(8,128)(2,1)S(1)}, u32[]{:S(2)}, u32[]{:S(2)}) collective-permute-start(bf16[5,1,80,640]{3,2,1,0:T(8,128)(2,1)S(1)} %add.54.refs_11_), channel_id=1, source_target_pairs={{0,1},{1,0},{2,3},{3,2},{4,5},{5,4},{6,7},{7,6},{8,9},{9,8},{10,11... | collective-permute-start | bytes 1536008 | tf_op jit(solution)/shard_map/ppermute | solution.py:387
  97.0 17.2 %collective-permute-start.4 = (bf16[1,4,32,1920]{3,2,1,0:T(8,128)(2,1)}, bf16[1,4,32,1920]{3,2,1,0:T(8,128)(2,1)S(1)}, u32[]{:S(2)}, u32[]{:S(2)}) collective-permute-start(bf16[1,4,32,1920]{3,2,1,0:T(8,128)(2,1)} %slice.4), channel_id=1, source_target_pairs={{0,1},{1,2},{2,3},{4,5},{5,6},{6,7},{8,9},{9,10},{10,11},{12,13},{... | collective-permute-start | bytes 1474568 | tf_op jit(solution)/shard_map/ppermute | solution.py:20
  101.5 12.7 %collective-permute-start.12 = (bf16[4,1,80,640]{3,2,1,0:T(8,128)(2,1)}, bf16[4,1,80,640]{3,2,1,0:T(8,128)(2,1)S(1)}, u32[]{:S(2)}, u32[]{:S(2)}) collective-permute-start(bf16[4,1,80,640]{3,2,1,0:T(8,128)(2,1)} %collective-permute-done.10.refs_4_), channel_id=1, source_target_pairs={{0,1},{1,0},{2,3},{3,2},{4,5},{5,4},{6,7},{7,6},{8,9},{9,8},{10,11... | collective-permute-start | bytes 1228808 | tf_op jit(solution)/shard_map/ppermute | solution.py:387
  102.7 11.5 %collective-permute-start.16 = (bf16[4,1,80,640]{3,2,1,0:T(8,128)(2,1)S(1)}, bf16[4,1,80,640]{3,2,1,0:T(8,128)(2,1)}, u32[]{:S(2)}, u32[]{:S(2)}) collective-permute-start(bf16[4,1,80,640]{3,2,1,0:T(8,128)(2,1)S(1)} %collective-permute-done.14.refs_8_), channel_id=1, source_target_pairs={{0,1},{1,0},{2,3},{3,2},{4,5},{5,4},{6,7},{7,6},{8,9},{9,8},{10,11... | collective-permute-start | bytes 1228808 | tf_op jit(solution)/shard_map/ppermute | solution.py:387
  102.8 11.5 %collective-permute-start.21 = (bf16[4,1,80,640]{3,2,1,0:T(8,128)(2,1)}, bf16[4,1,80,640]{3,2,1,0:T(8,128)(2,1)}, u32[]{:S(2)}, u32[]{:S(2)}) collective-permute-start(bf16[4,1,80,640]{3,2,1,0:T(8,128)(2,1)} %collective-permute-done.19.refs_12_), channel_id=1, source_target_pairs={{0,1},{1,0},{2,3},{3,2},{4,5},{5,4},{6,7},{7,6},{8,9},{9,8},{10,11... | collective-permute-start | bytes 1228808 | tf_op jit(solution)/shard_map/ppermute | solution.py:387
  126.9 23.2 %all-to-all-start = ((bf16[8,4,16,640]{3,2,1,0:T(8,128)(2,1)}), bf16[8,4,16,640]{3,2,1,0:T(8,128)(2,1)S(1)}, u32[]{:S(2)}, u32[]{:S(2)}) async-start(bf16[8,4,16,640]{3,2,1,0:T(8,128)(2,1)} %shard_map.120), calls=%async_computation | async-start | bytes 1310720 | tf_op jit(solution)/shard_map/all_to_all | solution.py:345
  132.6 21.2 %copy-start.13 = (f32[1280]{0:T(1024)S(1)}, f32[1280]{0:T(1024)}, u32[]{:S(2)}) copy-start(f32[1280]{0:T(1024)} %param.17) | copy-start | bytes 15364
  132.6 21.8 %copy-start.14 = (f32[1280]{0:T(1024)S(1)}, f32[1280]{0:T(1024)}, u32[]{:S(2)}) copy-start(f32[1280]{0:T(1024)} %param.22) | copy-start | bytes 15364
  150.1 21.1 %all-to-all-start.2 = ((bf16[8,4,16,640]{3,2,1,0:T(8,128)(2,1)}), bf16[8,4,16,640]{3,2,1,0:T(8,128)(2,1)S(1)}, u32[]{:S(2)}, u32[]{:S(2)}) async-start(bf16[8,4,16,640]{3,2,1,0:T(8,128)(2,1)} %shard_map.122), calls=%async_computation.2 | async-start | bytes 1310720 | tf_op jit(solution)/shard_map/all_to_all | solution.py:345
  171.2 21.1 %all-to-all-start.1 = ((bf16[8,2,16,1280]{3,2,1,0:T(8,128)(2,1)}), bf16[8,2,16,1280]{3,2,1,0:T(8,128)(2,1)S(1)}, u32[]{:S(2)}, u32[]{:S(2)}) async-start(bf16[8,2,16,1280]{3,2,1,0:T(8,128)(2,1)} %bitcast.19), calls=%async_computation.1 | async-start | bytes 1310720 | tf_op jit(solution)/shard_map/all_to_all | solution.py:349
  (9 other events, 60.6 us)
